TPU v7x, 32 devices: a whole 2x2x4 slice. The times are simulated.
32 devices in a mesh: dp: 8 (over z, core), tensor: 4 (over y, x).
Axes of the slice: x: 2, y: 2, z: 4, core: 2. Of those that a mesh axis runs over, the one named last changes fastest.
Arguments:
- hidden_in: bfloat16 [2048, 8192], P(('dp', 'tensor')), may hold values from -6 to 6
- out_grad: bfloat16 [2048, 8192], P(('dp', 'tensor')), may hold values from -0.29882812 to 0.29882812
- seq_lengths: int32 [8, 8], P('dp'), may hold values from 1 to 128, 256 in all within a row
- seq_adapter: int32 [8, 8], P('dp'), may hold values from 0 to 15
- query_weight: bfloat16 [8192, 4096], P(None, 'tensor'), may hold values from -0.0625 to 0.0625
- key_value_weight: bfloat16 [2, 8192, 1024], P(None, None, 'tensor'), may hold values from -0.0625 to 0.0625
- output_weight: bfloat16 [4096, 8192], P('tensor'), may hold values from -0.09375 to 0.09375
- a_in: bfloat16 [16, 48, 8192], P('dp', None, 'tensor'), may hold values from -0.0625 to 0.0625
- b_query: bfloat16 [16, 16, 4096], P('dp', None, 'tensor'), may hold values from -0.375 to 0.375
- b_key_value: bfloat16 [16, 2, 16, 1024], P('dp', None, None, 'tensor'), may hold values from -0.375 to 0.375
- output_down_factor: bfloat16 [16, 16, 4096], P('dp', None, 'tensor'), may hold values from -0.09375 to 0.09375
- output_up_factor: bfloat16 [16, 16, 8192], P('dp', 'tensor'), may hold values from -0.375 to 0.375
Outputs:
- attn_out: bfloat16 [2048, 8192], P(('dp', 'tensor'))
- input_grad: bfloat16 [2048, 8192], P(('dp', 'tensor'))
- input_down_gradient: float32 [16, 48, 8192], P('dp', None, 'tensor')
- query_up_gradient: float32 [16, 16, 4096], P('dp', None, 'tensor')
- grad_b_key_value: float32 [16, 2, 16, 1024], P('dp', None, None, 'tensor')
- output_down_gradient: float32 [16, 16, 4096], P('dp', None, 'tensor')
- output_up_gradient: float32 [16, 16, 8192], P('dp', 'tensor')
All inputs are finite; a program needn't handle non-finite values.
Results may differ from a plain program's by a relative error of at most 0.015.
Values may be sent and summed in bfloat16 or wider, within the bound.
A program may use at most 192 MiB of HBM per device.

v0:
```python
import jax
import jax.numpy as jnp
from jax import lax
from jax.sharding import PartitionSpec as P

HEAD_SIZE = 128


adapter_scale = 2.0
rope_theta = 500000.0
masked_score = -1e30


def contract_trailing_axis(left, right):
    return lax.dot_general(
        left, right, (((1,), (1,)), ((), ())), preferred_element_type=jnp.float32
    )


def contract_leading_axis(left, right):
    return lax.dot_general(
        left, right, (((0,), (0,)), ((), ())), preferred_element_type=jnp.float32
    )


def token_tables(lengths, adapters, tok_total, adapter_overall_count):
    seq_ends = jnp.cumsum(lengths)
    seq_starts = seq_ends - lengths
    token_ids = jnp.arange(tok_total, dtype=jnp.int32)
    member = (
        (token_ids[:, None] >= seq_starts[None, :]) & (token_ids[:, None] < seq_ends[None, :])
    ).astype(jnp.int32)
    seq_index = jnp.sum(member * jnp.arange(lengths.shape[0], dtype=jnp.int32)[None, :], axis=1)
    position = token_ids - jnp.sum(member * seq_starts[None, :], axis=1)
    adapter_of = jnp.sum(member * adapters[None, :], axis=1)
    adapter_hot = adapter_of[:, None] == jnp.arange(adapter_overall_count, dtype=jnp.int32)[None, :]
    allowed = (seq_index[:, None] == seq_index[None, :]) & (
        token_ids[None, :] <= token_ids[:, None]
    )
    return (position, adapter_hot, allowed)


def rope_tables(position):
    half_dim = HEAD_SIZE // 2
    inverse = rope_theta ** (-(jnp.arange(half_dim, dtype=jnp.float32) * (2.0 / HEAD_SIZE)))
    angle = position.astype(jnp.float32)[:, None] * inverse[None, :]
    cosine_table = jnp.concatenate([jnp.cos(angle), jnp.cos(angle)], axis=1)
    sine_table = jnp.concatenate([jnp.sin(angle), jnp.sin(angle)], axis=1)
    return (cosine_table, sine_table)


def apply_rotation(vectors, cosine_table, sine_table):
    half_dim = HEAD_SIZE // 2
    turned = jnp.concatenate([-vectors[..., half_dim:], vectors[..., :half_dim]], axis=-1)
    return vectors * cosine_table[:, None, :] + turned * sine_table[:, None, :]


def choose_rank_rows(onehot_single, product, rank_width):
    shaped = product.reshape(product.shape[0], onehot_single.shape[1], rank_width)
    return jnp.sum(shaped * onehot_single[:, :, None], axis=1)


def expand_from_rank(onehot_halfprec, factors):
    return (onehot_halfprec[:, :, None] * factors[:, None, :]).reshape(
        factors.shape[0], onehot_halfprec.shape[1] * factors.shape[1]
    )


def attend(queries, rotated_keys, incoming_values, allowed):
    tok_total, head_count, _ = queries.shape
    group_count = rotated_keys.shape[1]
    per_group = head_count // group_count
    grouped = queries.reshape(tok_total, group_count, per_group, HEAD_SIZE)
    scores = jnp.einsum(
        "tgpe,sge->gpts", grouped, rotated_keys, preferred_element_type=jnp.float32
    ) * HEAD_SIZE ** (-0.5)
    scores = jnp.where(allowed[None, None], scores, masked_score)
    peak = jnp.max(scores, axis=-1, keepdims=True)
    expped = jnp.exp(scores - peak)
    probs = expped / jnp.sum(expped, axis=-1, keepdims=True)
    probs_bf = probs.astype(jnp.bfloat16)
    blended_output = jnp.einsum(
        "gpts,sge->tgpe", probs_bf, incoming_values, preferred_element_type=jnp.float32
    )
    return (
        blended_output.reshape(tok_total, head_count * HEAD_SIZE).astype(jnp.bfloat16),
        probs,
        probs_bf,
    )


def attend_back(queries, rotated_keys, incoming_values, probs, probs_bf, blended_gradient):
    tok_total, head_count, _ = queries.shape
    group_count = rotated_keys.shape[1]
    per_group = head_count // group_count
    incoming_gradient = blended_gradient.reshape(tok_total, group_count, per_group, HEAD_SIZE)
    grad_probs = jnp.einsum(
        "tgpe,sge->gpts", incoming_gradient, incoming_values, preferred_element_type=jnp.float32
    )
    grad_values = jnp.einsum(
        "gpts,tgpe->sge", probs_bf, incoming_gradient, preferred_element_type=jnp.float32
    )
    inner = jnp.sum(grad_probs * probs, axis=-1, keepdims=True)
    grad_scores = (probs * (grad_probs - inner) * HEAD_SIZE ** (-0.5)).astype(jnp.bfloat16)
    grouped = queries.reshape(tok_total, group_count, per_group, HEAD_SIZE)
    grad_queries = jnp.einsum(
        "gpts,sge->tgpe", grad_scores, rotated_keys, preferred_element_type=jnp.float32
    )
    grad_keys = jnp.einsum(
        "gpts,tgpe->sge", grad_scores, grouped, preferred_element_type=jnp.float32
    )
    return (grad_queries.reshape(tok_total, head_count, HEAD_SIZE), grad_keys, grad_values)


def local(
    hidden_in,
    out_grad,
    seq_lengths,
    seq_adapter,
    query_weight,
    key_value_weight,
    output_weight,
    a_in,
    b_query,
    b_key_value,
    output_down_factor,
    output_up_factor,
):
    mesh_parts = lax.axis_size("tensor")
    own_slot = lax.axis_index("tensor")
    tok_rows = hidden_in.shape[0]
    tok_total = tok_rows * mesh_parts
    full_width = hidden_in.shape[1]
    narrow_cast = full_width // mesh_parts
    adapter_rank_rows = output_down_factor.shape[1]
    rank_piece = output_up_factor.shape[1]
    query_columns = query_weight.shape[1]
    key_value_columns = key_value_weight.shape[2]
    input_down_every, query_up_every, key_value_up_every, output_down_every, b_out_all = (
        lax.all_gather(a_in, "dp", axis=0, tiled=True),
        lax.all_gather(b_query, "dp", axis=0, tiled=True),
        lax.all_gather(b_key_value, "dp", axis=0, tiled=True),
        lax.all_gather(output_down_factor, "dp", axis=0, tiled=True),
        lax.all_gather(output_up_factor, "dp", axis=0, tiled=True),
    )
    adapter_overall_count = input_down_every.shape[0]
    position, adapter_hot, allowed = token_tables(
        seq_lengths[0], seq_adapter[0], tok_total, adapter_overall_count
    )
    onehot_single = adapter_hot.astype(jnp.float32)
    onehot_halfprec = adapter_hot.astype(jnp.bfloat16)
    cosine_table, sine_table = rope_tables(position)
    input_down_flattened = input_down_every.reshape(
        adapter_overall_count * 3 * adapter_rank_rows, narrow_cast
    )
    query_up_flattened = query_up_every.reshape(
        adapter_overall_count * adapter_rank_rows, query_columns
    )
    key_up_flattened = key_value_up_every[:, 0].reshape(
        adapter_overall_count * adapter_rank_rows, key_value_columns
    )
    value_up_flattened = key_value_up_every[:, 1].reshape(
        adapter_overall_count * adapter_rank_rows, key_value_columns
    )
    output_down_flattened = output_down_every.reshape(
        adapter_overall_count * adapter_rank_rows, query_columns
    )
    output_up_flattened = b_out_all.reshape(adapter_overall_count * rank_piece, full_width)
    gathered = lax.all_gather(hidden_in, "tensor", axis=0, tiled=True)
    col_start = own_slot * narrow_cast
    local_columns = lax.dynamic_slice_in_dim(gathered, col_start, narrow_cast, 1)
    rank_partial_sum = choose_rank_rows(
        onehot_single,
        contract_trailing_axis(local_columns, input_down_flattened),
        3 * adapter_rank_rows,
    )
    input_rank_rows = lax.psum(rank_partial_sum, "tensor").astype(jnp.bfloat16)
    adapter_query_delta = expand_from_rank(onehot_halfprec, input_rank_rows[:, :adapter_rank_rows])
    adapter_key_delta = expand_from_rank(
        onehot_halfprec, input_rank_rows[:, adapter_rank_rows : 2 * adapter_rank_rows]
    )
    adapter_value_delta = expand_from_rank(
        onehot_halfprec, input_rank_rows[:, 2 * adapter_rank_rows :]
    )
    query_before_rotation = jnp.dot(
        gathered, query_weight, preferred_element_type=jnp.float32
    ) + adapter_scale * jnp.dot(
        adapter_query_delta, query_up_flattened, preferred_element_type=jnp.float32
    )
    key_before_rotation = jnp.dot(
        gathered, key_value_weight[0], preferred_element_type=jnp.float32
    ) + adapter_scale * jnp.dot(
        adapter_key_delta, key_up_flattened, preferred_element_type=jnp.float32
    )
    value_projected = jnp.dot(
        gathered, key_value_weight[1], preferred_element_type=jnp.float32
    ) + adapter_scale * jnp.dot(
        adapter_value_delta, value_up_flattened, preferred_element_type=jnp.float32
    )
    queries = apply_rotation(
        query_before_rotation.reshape(tok_total, query_columns // HEAD_SIZE, HEAD_SIZE),
        cosine_table,
        sine_table,
    ).astype(jnp.bfloat16)
    rotated_keys = apply_rotation(
        key_before_rotation.reshape(tok_total, key_value_columns // HEAD_SIZE, HEAD_SIZE),
        cosine_table,
        sine_table,
    ).astype(jnp.bfloat16)
    incoming_values = value_projected.reshape(
        tok_total, key_value_columns // HEAD_SIZE, HEAD_SIZE
    ).astype(jnp.bfloat16)
    blended_output, probs, probs_bf = attend(queries, rotated_keys, incoming_values, allowed)
    output_partial_sum = choose_rank_rows(
        onehot_single,
        contract_trailing_axis(blended_output, output_down_flattened),
        adapter_rank_rows,
    )
    output_rank_rows = lax.psum(output_partial_sum, "tensor").astype(jnp.bfloat16)
    adapter_output_delta = expand_from_rank(
        onehot_halfprec,
        lax.dynamic_slice_in_dim(output_rank_rows, own_slot * rank_piece, rank_piece, 1),
    )
    adapter_row_values = adapter_output_delta
    attn_out = lax.psum_scatter(
        (
            jnp.dot(blended_output, output_weight, preferred_element_type=jnp.float32)
            + adapter_scale
            * jnp.dot(adapter_row_values, output_up_flattened, preferred_element_type=jnp.float32)
        ).astype(jnp.bfloat16),
        "tensor",
        scatter_dimension=0,
        tiled=True,
    )
    incoming_gradient = lax.all_gather(out_grad, "tensor", axis=0, tiled=True)
    grad_part = (
        adapter_scale
        * choose_rank_rows(
            onehot_single,
            contract_trailing_axis(incoming_gradient, output_up_flattened),
            rank_piece,
        )
    ).astype(jnp.bfloat16)
    output_rank_gradient = lax.all_gather(grad_part, "tensor", axis=1, tiled=True)
    output_up_gradient = (
        adapter_scale * contract_leading_axis(adapter_output_delta, incoming_gradient)
    ).reshape(adapter_overall_count, rank_piece, full_width)
    adapter_output_gradient = expand_from_rank(onehot_halfprec, output_rank_gradient)
    blended_gradient = (
        contract_trailing_axis(incoming_gradient, output_weight)
        + jnp.dot(
            adapter_output_gradient, output_down_flattened, preferred_element_type=jnp.float32
        )
    ).astype(jnp.bfloat16)
    output_down_gradient = contract_leading_axis(adapter_output_gradient, blended_output).reshape(
        adapter_overall_count, adapter_rank_rows, query_columns
    )
    grad_queries, grad_keys, grad_values = attend_back(
        queries, rotated_keys, incoming_values, probs, probs_bf, blended_gradient
    )
    query_gradient_rows = (
        apply_rotation(grad_queries, cosine_table, -sine_table)
        .reshape(tok_total, query_columns)
        .astype(jnp.bfloat16)
    )
    key_gradient_rows = (
        apply_rotation(grad_keys, cosine_table, -sine_table)
        .reshape(tok_total, key_value_columns)
        .astype(jnp.bfloat16)
    )
    value_gradient_rows = grad_values.reshape(tok_total, key_value_columns).astype(jnp.bfloat16)
    backward_partial_sum = jnp.concatenate(
        [
            choose_rank_rows(
                onehot_single,
                contract_trailing_axis(query_gradient_rows, query_up_flattened),
                adapter_rank_rows,
            ),
            choose_rank_rows(
                onehot_single,
                contract_trailing_axis(key_gradient_rows, key_up_flattened),
                adapter_rank_rows,
            ),
            choose_rank_rows(
                onehot_single,
                contract_trailing_axis(value_gradient_rows, value_up_flattened),
                adapter_rank_rows,
            ),
        ],
        axis=1,
    )
    input_rank_gradient = (adapter_scale * lax.psum(backward_partial_sum, "tensor")).astype(
        jnp.bfloat16
    )
    query_up_gradient = (
        adapter_scale * contract_leading_axis(adapter_query_delta, query_gradient_rows)
    ).reshape(adapter_overall_count, adapter_rank_rows, query_columns)
    key_up_gradient = (
        adapter_scale * contract_leading_axis(adapter_key_delta, key_gradient_rows)
    ).reshape(adapter_overall_count, adapter_rank_rows, key_value_columns)
    value_up_gradient = (
        adapter_scale * contract_leading_axis(adapter_value_delta, value_gradient_rows)
    ).reshape(adapter_overall_count, adapter_rank_rows, key_value_columns)
    grad_b_kv = jnp.stack([key_up_gradient, value_up_gradient], axis=1)
    adapter_input_gradient = expand_from_rank(onehot_halfprec, input_rank_gradient)
    input_down_gradient = contract_leading_axis(adapter_input_gradient, local_columns).reshape(
        adapter_overall_count, 3 * adapter_rank_rows, narrow_cast
    )
    adapter_row_values = adapter_input_gradient
    heads_sum = contract_trailing_axis(query_gradient_rows, query_weight) + contract_trailing_axis(
        key_gradient_rows, key_value_weight[0]
    )
    heads_sum = heads_sum + contract_trailing_axis(value_gradient_rows, key_value_weight[1])
    adjacent_columns = jnp.dot(
        adapter_row_values, input_down_flattened, preferred_element_type=jnp.float32
    )
    placed = lax.dynamic_update_slice_in_dim(
        jnp.zeros((lax.axis_size("tensor") * tok_rows, full_width), jnp.float32),
        adjacent_columns,
        col_start,
        1,
    )
    input_grad = lax.psum_scatter(
        (heads_sum + placed).astype(jnp.bfloat16), "tensor", scatter_dimension=0, tiled=True
    )
    summed_a_in, summed_b_query, summed_b_kv, summed_a_out, summed_b_out = (
        lax.psum_scatter(input_down_gradient, "dp", scatter_dimension=0, tiled=True),
        lax.psum_scatter(query_up_gradient, "dp", scatter_dimension=0, tiled=True),
        lax.psum_scatter(grad_b_kv, "dp", scatter_dimension=0, tiled=True),
        lax.psum_scatter(output_down_gradient, "dp", scatter_dimension=0, tiled=True),
        lax.psum_scatter(output_up_gradient, "dp", scatter_dimension=0, tiled=True),
    )
    return (
        attn_out,
        input_grad,
        summed_a_in,
        summed_b_query,
        summed_b_kv,
        summed_a_out,
        summed_b_out,
    )


def solution(mesh):
    in_specs = (
        P(("dp", "tensor"), None),
        P(("dp", "tensor"), None),
        P("dp", None),
        P("dp", None),
        P(None, "tensor"),
        P(None, None, "tensor"),
        P("tensor", None),
        P("dp", None, "tensor"),
        P("dp", None, "tensor"),
        P("dp", None, None, "tensor"),
        P("dp", None, "tensor"),
        P("dp", "tensor", None),
    )
    out_specs = (
        P(("dp", "tensor"), None),
        P(("dp", "tensor"), None),
        P("dp", None, "tensor"),
        P("dp", None, "tensor"),
        P("dp", None, None, "tensor"),
        P("dp", None, "tensor"),
        P("dp", "tensor", None),
    )
    return jax.shard_map(local, mesh=mesh, in_specs=in_specs, out_specs=out_specs, check_vma=False)
```

profile of v0, /device:TPU:23, one launch (start us, length us, event | category | flops | bytes accessed | tf_op | source)
XLA Modules:
  0.0 611.8 jit_solution(17167570973509118959)
XLA Ops:
  7.2 0.7 all-gather.10.cloned.1.call-update
  8.0 0.7 all-gather.12.cloned.1.call-update
  8.7 0.7 all-gather.8.cloned.1.call-update
  10.0 0.8 reduce-window.4
  10.9 0.8 copy.119
  11.6 13.7 %all_gather.26 = bf16[16,2,16,256]{3,2,0,1:T(8,128)(2,1)S(1)} all-gather(bf16[2,2,16,256]{3,2,0,1:T(8,128)(2,1)S(1)} %copy.119), channel_id=1, replica_groups=mesh['dp'=8,'tensor'=4] {'dp'}, dimensions={0}, use_global_device_ids=true | all-gather | bytes 294912 | tf_op jit(solution)/shard_map/all_gather | solution.py:142
  25.4 0.7 fusion.88
  26.0 0.7 select_reduce_fusion
  27.2 0.7 fusion.64
  27.9 15.0 %all_gather.27 = bf16[16,16,1024]{2,1,0:T(8,128)(2,1)S(1)} all-gather(bf16[2,16,1024]{2,1,0:T(8,128)(2,1)} %param.20), channel_id=1, replica_groups=mesh['dp'=8,'tensor'=4] {'dp'}, dimensions={0}, use_global_device_ids=true | all-gather | bytes 589824 | tf_op jit(solution)/shard_map/all_gather | solution.py:141
  42.9 15.1 %all_gather.28 = bf16[16,16,1024]{2,1,0:T(8,128)(2,1)S(1)} all-gather(bf16[2,16,1024]{2,1,0:T(8,128)(2,1)S(1)} %copy-done.22), channel_id=1, replica_groups=mesh['dp'=8,'tensor'=4] {'dp'}, dimensions={0}, use_global_device_ids=true | all-gather | bytes 589824 | tf_op jit(solution)/shard_map/all_gather | solution.py:143
  58.1 28.8 %all-gather.12.cloned.1.call-done = bf16[256,8192]{1,0:T(8,128)(2,1)} async-done(((bf16[64,8192]{1,0:T(8,128)(2,1)}), bf16[256,8192]{1,0:T(8,128)(2,1)}) %all-gather.12.cloned.1.call-update) | async-done | bytes 4194320 | tf_op jit(solution)/shard_map/all_gather | solution.py:235
  87.0 3.9 fusion.36
  90.9 6.0 all-gather
  96.9 30.2 %all-gather.8.cloned.1.call-done = bf16[16,48,2048]{2,1,0:T(8,128)(2,1)} async-done(((bf16[2,48,2048]{2,1,0:T(8,128)(2,1)}), bf16[16,48,2048]{2,1,0:T(8,128)(2,1)}) %all-gather.8.cloned.1.call-update) | async-done | bytes 3145744 | tf_op jit(solution)/shard_map/all_gather | solution.py:140
  127.1 53.1 %all-gather.6.cloned.1.call-done = bf16[256,8192]{1,0:T(8,128)(2,1)} async-done(((bf16[64,8192]{1,0:T(8,128)(2,1)}), bf16[256,8192]{1,0:T(8,128)(2,1)}) %all-gather.6.cloned.1.call-update) | async-done | bytes 4194320 | tf_op jit(solution)/shard_map/all_gather | solution.py:169
  180.2 3.2 fusion.24
  183.5 11.9 %psum.21 = bf16[256,48]{0,1:T(8,128)(2,1)S(1)} all-reduce(f32[256,48]{0,1:T(8,128)S(1)} %fusion.24), channel_id=1, replica_groups=mesh['dp'=8,'tensor'=4] {'tensor'}, use_global_device_ids=true, to_apply=%region_3.4 | all-reduce | flops 12288 | bytes 73728 | tf_op jit(solution)/shard_map/psum | solution.py:177
  195.4 0.7 broadcast_multiply_fusion.1
  196.1 5.2 fusion.7
  201.5 0.7 slice_negate_fusion.3
  202.6 1.0 copy-done.19
  203.5 9.4 %convolution_add_fusion.4 = f32[256,1024]{1,0:T(8,128)} fusion(f32[256,1024]{1,0:T(8,128)S(1)} %fusion.22, bf16[256,8192]{1,0:T(8,128)(2,1)S(1)} %copy-done.19, bf16[8192,1024]{1,0:T(8,128)(2,1)} %param.16), kind=kOutput, calls=%fused_computation.33 | convolution fusion | flops 4295229440 | bytes 23068672 | tf_op jit(solution)/shard_map/dot_general | solution.py:185
  213.0 1.6 copy.164
  214.6 1.3 convolution_bitcast_fusion.2
  215.9 11.7 %fusion.23 = bf16[256,1024]{1,0:T(8,128)(2,1)S(1)} fusion(f32[256,1024]{1,0:T(8,128)} %convolution_bitcast_fusion.2, bf16[256,8192]{1,0:T(8,128)(2,1)} %all-gather.12.cloned.1.call-done, bf16[1024,8192]{1,0:T(8,128)(2,1)} %param.18), kind=kOutput, calls=%fused_computation.40 | convolution fusion | flops 4295491584 | bytes 22544384 | tf_op jit(solution)/shard_map/dot_general | solution.py:15
  227.9 5.2 fusion.10
  233.1 0.9 fusion.27
  234.1 1.0 fusion.40
  235.1 3.2 fusion.99
  238.3 2.2 fusion.28
  240.9 1.8 fusion.100
  242.8 4.3 convolution_bitcast_fusion.5
  247.1 4.3 fusion.51
  251.3 0.8 fusion.32
  252.4 0.9 copy.141
  253.2 1.3 fusion.29
  255.1 0.8 copy.139
  256.0 1.2 broadcast_multiply_fusion
  258.0 12.0 %all-reduce.3 = (bf16[256,16]{0,1:T(8,128)(2,1)S(1)}, f32[256,48]{0,1:T(8,128)S(1)}) all-reduce(f32[256,16]{0,1:T(8,128)S(1)} %fusion.29, f32[256,48]{0,1:T(8,128)S(1)} %pad_maximum_fusion.4), channel_id=1, replica_groups=mesh['dp'=8,'tensor'=4] {'tensor'}, use_global_device_ids=true, to_apply=%region_9.10 | all-reduce | flops 16384 | bytes 122880 | tf_op jit(solution)/shard_map/psum | solution.py:219
  270.1 3.0 convolution_multiply_fusion
  273.2 1.7 reshape.308
  274.8 1.9 pad_maximum_fusion.1
  276.9 2.4 fusion.72
  279.4 1.4 convolution_multiply_fusion.1
  280.9 1.3 fusion.2
  282.2 12.3 %fusion.3 = bf16[256,8192]{1,0:T(8,128)(2,1)} fusion(f32[256,8192]{1,0:T(8,128)S(1)} %fusion.2, bf16[256,1024]{0,1:T(8,128)(2,1)S(1)} %bitcast.233, bf16[1024,8192]{1,0:T(8,128)(2,1)} %param.18), kind=kOutput, calls=%fused_computation.7 | convolution fusion | flops 4299161600 | bytes 29884416 | tf_op jit(solution)/shard_map/dot_general | solution.py:227
  294.6 1.2 copy-done
  295.9 19.5 %fusion.101 = f32[256,8192]{1,0:T(8,128)} fusion(bf16[256,1024]{0,1:T(8,128)(2,1)S(1)} %fusion.42, bf16[8192,1024]{1,0:T(8,128)(2,1)} %param.16), kind=kOutput, calls=%fused_computation.162 | convolution fusion | flops 4294967296 | bytes 25690112 | tf_op jit(solution)/shard_map/dot_general | solution.py:15
  315.4 6.1 convolution_add_fusion.1
  321.5 3.8 convolution_add_fusion
  325.3 1.2 fusion.17
  326.5 2.5 convert_element_type.128
  329.1 4.9 fusion.45
  334.0 0.6 copy-done.27
  335.9 17.7 %all-reduce.6.cloned.1.call-done = (f32[16,2,16,256]{3,2,0,1:T(8,128)}, f32[16,4,8192]{2,1,0:T(4,128)}) async-done(((f32[16,2,16,256]{3,2,0,1:T(8,128)}, f32[16,4,8192]{2,1,0:T(4,128)}), (f32[16,2,16,256]{3,2,0,1:T(8,128)}, f32[16,4,8192]{2,1,0:T(4,128)})) %all-reduce.6.cloned.1.call-update) | async-done | bytes 2621456
  353.6 0.8 constant_dynamic-slice_fusion.1
  354.5 0.6 copy.143
  355.1 1.7 constant_dynamic-slice_fusion
  356.8 27.1 %reduce-scatter.17.cloned.1.call-done = f32[2,16,1024]{2,1,0:T(8,128)} async-done(((f32[16,16,1024]{2,1,0:T(8,128)}), f32[2,16,1024]{2,1,0:T(8,128)}) %reduce-scatter.17.cloned.1.call-update) | async-done | bytes 131088 | tf_op jit(solution)/shard_map/reduce_scatter | solution.py:330
  383.9 33.5 %reduce-scatter.15.cloned.1.call-done = f32[2,16,1024]{2,1,0:T(8,128)} async-done(((f32[16,16,1024]{2,1,0:T(8,128)}), f32[2,16,1024]{2,1,0:T(8,128)}) %reduce-scatter.15.cloned.1.call-update) | async-done | bytes 131088 | tf_op jit(solution)/shard_map/reduce_scatter | solution.py:328
  417.4 58.7 %reduce-scatter.9.cloned.1.call-done = bf16[64,8192]{1,0:T(8,128)(2,1)} async-done(((bf16[256,8192]{1,0:T(8,128)(2,1)}), bf16[64,8192]{1,0:T(8,128)(2,1)}) %reduce-scatter.9.cloned.1.call-update) | async-done | bytes 1048592 | tf_op jit(solution)/shard_map/reduce_scatter | solution.py:225
  476.1 56.6 %reduce-scatter.11.cloned.1.call-done = bf16[64,8192]{1,0:T(8,128)(2,1)} async-done(((bf16[256,8192]{1,0:T(8,128)(2,1)}), bf16[64,8192]{1,0:T(8,128)(2,1)}) %reduce-scatter.11.cloned.1.call-update) | async-done | bytes 1048592 | tf_op jit(solution)/shard_map/reduce_scatter | solution.py:323
  532.6 71.8 %reduce-scatter.13.cloned.1.call-done = f32[2,48,2048]{2,1,0:T(8,128)} async-done(((f32[16,48,2048]{2,1,0:T(8,128)}), f32[2,48,2048]{2,1,0:T(8,128)}) %reduce-scatter.13.cloned.1.call-update) | async-done | bytes 786448 | tf_op jit(solution)/shard_map/reduce_scatter | solution.py:327
  (106 shorter events, 5.1 us)
Async XLA Ops:
  7.2 35.8 %copy-start.22 = (bf16[2,16,1024]{2,1,0:T(8,128)(2,1)S(1)}, bf16[2,16,1024]{2,1,0:T(8,128)(2,1)}, u32[]{:S(2)}) copy-start(bf16[2,16,1024]{2,1,0:T(8,128)(2,1)} %param.22) | copy-start | bytes 196612
  7.2 50.9 %all-gather.10.cloned.1.call-start = ((), (), s32[]{:S(2)}) async-start(), calls=%async_computation.7 | async-start | bytes 1179648 | tf_op jit(solution)/shard_map/all_gather | solution.py:144
  7.9 79.0 %all-gather.12.cloned.1.call-start = ((), (), s32[]{:S(2)}) async-start(), calls=%async_computation.9 | async-start | bytes 5242880 | tf_op jit(solution)/shard_map/all_gather | solution.py:235
  8.7 118.4 %all-gather.8.cloned.1.call-start = ((), (), s32[]{:S(2)}) async-start(), calls=%async_computation.6 | async-start | bytes 3538944 | tf_op jit(solution)/shard_map/all_gather | solution.py:140
  9.4 170.8 %all-gather.6.cloned.1.call-start = ((), (), s32[]{:S(2)}) async-start(), calls=%async_computation.5 | async-start | bytes 5242880 | tf_op jit(solution)/shard_map/all_gather | solution.py:169
  10.0 343.6 %all-reduce.6.cloned.1.call-start = ((), (), s32[]{:S(2)}) async-start(), calls=%async_computation.14 | async-start | bytes 5242880
  25.4 226.0 %copy-start.7 = (bf16[16,2,16,256]{3,2,0,1:T(8,128)(2,1)}, bf16[16,2,16,256]{3,2,0,1:T(8,128)(2,1)S(1)}, u32[]{:S(2)}) copy-start(bf16[16,2,16,256]{3,2,0,1:T(8,128)(2,1)S(1)} %all_gather.26) | copy-start | bytes 786436
  27.1 153.1 %copy-start.23 = (f32[256,16]{0,1:T(8,128)}, f32[256,16]{0,1:T(8,128)S(1)}, u32[]{:S(2)}) copy-start(f32[256,16]{0,1:T(8,128)S(1)} %get-tuple-element.65) | copy-start | bytes 49156
  42.9 159.3 %copy-start.11 = (bf16[16,16,1024]{2,1,0:T(8,128)(2,1)}, bf16[16,16,1024]{2,1,0:T(8,128)(2,1)S(1)}, u32[]{:S(2)}) copy-start(bf16[16,16,1024]{2,1,0:T(8,128)(2,1)S(1)} %all_gather.27) | copy-start | bytes 1572868
  58.1 156.5 %copy-start.13 = (bf16[16,16,1024]{2,1,0:T(8,128)(2,1)}, bf16[16,16,1024]{2,1,0:T(8,128)(2,1)S(1)}, u32[]{:S(2)}) copy-start(bf16[16,16,1024]{2,1,0:T(8,128)(2,1)S(1)} %all_gather.28) | copy-start | bytes 1572868
  201.3 2.3 copy-start.19
  227.9 6.2 %copy-start.14 = (f32[256,2,64]{0,2,1:T(8,128)S(1)}, f32[256,2,64]{0,2,1:T(8,128)}, u32[]{:S(2)}) copy-start(f32[256,2,64]{0,2,1:T(8,128)} %get-tuple-element.50) | copy-start | bytes 393220
  227.9 6.1 %copy-start.15 = (f32[256,2,64]{0,2,1:T(8,128)S(1)}, f32[256,2,64]{0,2,1:T(8,128)}, u32[]{:S(2)}) copy-start(f32[256,2,64]{0,2,1:T(8,128)} %get-tuple-element.51) | copy-start | bytes 393220
  234.1 4.2 copy-start.20
  238.3 4.5 copy-start.29
  238.3 2.3 copy-start.18
  238.3 2.3 copy-start.28
  240.6 11.6 %copy-start.9 = (bf16[2,128,256]{2,1,0:T(8,128)(2,1)}, bf16[2,128,256]{2,1,0:T(8,128)(2,1)S(1)}, u32[]{:S(2)}) copy-start(bf16[2,128,256]{2,1,0:T(8,128)(2,1)S(1)} %fusion.28) | copy-start | bytes 393220
  240.6 2.2 copy-start.16
  240.9 12.3 %copy-start.2 = (bf16[2,128,4,256]{3,1,2,0:T(8,128)(2,1)}, bf16[2,128,4,256]{3,1,2,0:T(8,128)(2,1)S(1)}, u32[]{:S(2)}) copy-start(bf16[2,128,4,256]{3,1,2,0:T(8,128)(2,1)S(1)} %convolution_convert_fusion) | copy-start | bytes 1572868
  242.8 4.3 copy-start.21
  247.0 4.3 copy-start.24
  252.1 2.5 copy-start.8
  256.0 1.5 copy-start.12
  256.0 1.5 copy-start.25
  257.2 0.8 copy-start.26
  257.4 12.7 %copy-start.4 = (bf16[256,2,4,128]{0,3,2,1:T(8,128)(2,1)}, bf16[256,2,4,128]{0,3,2,1:T(8,128)(2,1)S(1)}, u32[]{:S(2)}) copy-start(bf16[256,2,4,128]{0,3,2,1:T(8,128)(2,1)S(1)} %fusion.44) | copy-start | bytes 1572868
  274.8 4.5 copy-start.5
  274.8 4.5 copy-start.17
  276.8 4.1 copy-start.6
  276.8 107.1 %reduce-scatter.17.cloned.1.call-start = ((), (), s32[]{:S(2)}) async-start(), calls=%async_computation.13 | async-start | bytes 1179648 | tf_op jit(solution)/shard_map/reduce_scatter | solution.py:330
  279.3 138.1 %reduce-scatter.15.cloned.1.call-start = ((), (), s32[]{:S(2)}) async-start(), calls=%async_computation.12 | async-start | bytes 1179648 | tf_op jit(solution)/shard_map/reduce_scatter | solution.py:328
  280.8 1.4 copy-start.3
  280.8 195.3 %reduce-scatter.9.cloned.1.call-start = ((), (), s32[]{:S(2)}) async-start(), calls=%async_computation.8 | async-start | bytes 5242880 | tf_op jit(solution)/shard_map/reduce_scatter | solution.py:225
  294.5 1.2 copy-start
  294.5 238.1 %reduce-scatter.11.cloned.1.call-start = ((), (), s32[]{:S(2)}) async-start(), calls=%async_computation.10 | async-start | bytes 5242880 | tf_op jit(solution)/shard_map/reduce_scatter | solution.py:323
  315.4 6.1 copy-start.10
  321.5 3.8 copy-start.1
  329.0 275.4 %reduce-scatter.13.cloned.1.call-start = ((), (), s32[]{:S(2)}) async-start(), calls=%async_computation.11 | async-start | bytes 7077888 | tf_op jit(solution)/shard_map/reduce_scatter | solution.py:327
  334.0 0.7 copy-start.27
Sparse Core Ops, SparseCore 0:
  9.6 23.8 all-gather.9
  35.3 51.5 all-gather.11
  88.6 38.4 all-gather.7
  128.8 51.3 all-gather.5
  276.9 76.6 all-reduce.5
  356.3 27.5 reduce-scatter.16
  386.7 30.5 reduce-scatter.14
  420.9 55.1 reduce-scatter.8
  479.9 52.6 reduce-scatter.10
  535.4 69.0 reduce-scatter.12
where the time goes:
time: 622 us; the launch traced here: 612 us
  waiting for transfers between devices  380 us (61%)
  matrix products  117 us (19%)
  blocking collectives  73.8 us (12%)
  between operations  15.8 us (3%)
  local copies, waits for them, and re-layouts  12.6 us (2%)
  other arithmetic  12 us (2%)
    reduce_scatter x1, waiting for transfers between devices, local(): lax.psum_scatter(input_down_gradient, 'dp', scatter_dimension=0, tiled=True)  71.8 us
    reduce_scatter x1, waiting for transfers between devices, local(): lax.psum_scatter((jnp.dot(blended_output, output_weight, preferred_elemen...  58.7 us
    reduce_scatter x1, waiting for transfers between devices, local(): lax.psum_scatter((heads_sum + placed).astype(jnp.bfloat16), 'tensor', sca...  56.6 us
    all_gather x1, waiting for transfers between devices, local(): gathered = lax.all_gather(hidden_in, 'tensor', axis=0, tiled=True)  53.1 us
    dot_general x10, matrix products, contract_trailing_axis(): lax.dot_general(left, right, (((1,), (1,)), ((), ())), preferred_element_...  51.1 us
    reduce_scatter x1, waiting for transfers between devices, local(): lax.psum_scatter(query_up_gradient, 'dp', scatter_dimension=0, tiled=True)  33.5 us
    all_gather x1, waiting for transfers between devices, local(): lax.all_gather(a_in, 'dp', axis=0, tiled=True)  30.2 us
    all_gather x1, waiting for transfers between devices, local(): incoming_gradient = lax.all_gather(out_grad, 'tensor', axis=0, tiled=True)  28.8 us
  transfers between devices with their start and end apart: 10, of which 9 were waited for; matrix products, arithmetic and copies ran while one was open for 11% of the time, Pallas kernels for 0%

commit v1 on v0

--- a/solution.py
+++ b/solution.py
@@ -1,9 +1,561 @@
+import functools
+
 import jax
 import jax.numpy as jnp
 from jax import lax
+from jax.experimental import pallas as pl
+from jax.experimental.pallas import tpu as pltpu
 from jax.sharding import PartitionSpec as P
 
 HEAD_SIZE = 128
+
+
+MESH = pl.DeviceIdType.MESH
+VMEM_BYTES = 60 * 1024 * 1024
+ANY = pl.BlockSpec(memory_space=pl.ANY)
+VMEM = pl.BlockSpec(memory_space=pltpu.VMEM)
+
+
+def remote(src, dst, send_sem, recv_sem, device):
+    return pltpu.make_async_remote_copy(
+        src_ref=src,
+        dst_ref=dst,
+        send_sem=send_sem,
+        recv_sem=recv_sem,
+        device_id=device,
+        device_id_type=MESH,
+    )
+
+
+def tensor_peers(n):
+    me = lax.axis_index("tensor")
+    if n == 4:
+        across, up = lax.rem(me, 2), lax.div(me, 2)
+        return (me, up * 2 + 1 - across, (1 - up) * 2 + across, (1 - up) * 2 + 1 - across)
+    return (me,)
+
+
+def greet(devices):
+    barrier = pltpu.get_barrier_semaphore()
+    for device in devices:
+        pl.semaphore_signal(barrier, inc=1, device_id=device, device_id_type=MESH)
+    pl.semaphore_wait(barrier, len(devices))
+
+
+def tensor_devices(n):
+    if n == 4:
+        _, by_x, by_y, _ = tensor_peers(n)
+        return [{"tensor": by_x}, {"tensor": by_y}]
+    me = lax.axis_index("tensor")
+    return [{"tensor": lax.rem(me + k, n)} for k in range(1, n)]
+
+
+def dp_devices(total):
+    me = lax.axis_index("dp")
+    pairs = total // 2
+    spot, core = lax.div(me, 2), lax.rem(me, 2)
+    right = lax.rem(spot + 1, pairs) * 2 + core
+    left = lax.rem(spot + pairs - 1, pairs) * 2 + core
+    return [{"dp": spot * 2 + 1 - core}, {"dp": right}, {"dp": left}]
+
+
+def gather_kernel(n, total, nt, nd, *refs):
+    take = iter(refs)
+    t_in = [next(take) for _ in range(nt)]
+    d_in = [next(take) for _ in range(nd)]
+    t_out = [next(take) for _ in range(nt)]
+    d_out = [next(take) for _ in range(nd)]
+    stage = [next(take) for _ in range(nt + nd)]
+    load_sem, store_sem, t_send, t_recv, d_send, d_recv, s_send, s_recv = take
+    pairs = total // 2
+    me_dp = lax.axis_index("dp")
+    spot, core = lax.div(me_dp, 2), lax.rem(me_dp, 2)
+    sibling = {"dp": spot * 2 + 1 - core}
+    right, left = {"dp": (spot + 1) * 2 + core}, {"dp": (spot - 1) * 2 + core}
+    peers = tensor_peers(n)
+    me = peers[0]
+
+    greet(tensor_devices(n) + dp_devices(total))
+
+    def block(i, offset):
+        return d_out[i].at[(spot + offset) * 2 + core]
+
+    def to_side(i, direction, step):
+        source = d_in[i] if step == 0 else block(i, -step if direction == 0 else step)
+        target = block(i, -step if direction == 0 else step)
+        return remote(
+            source,
+            target,
+            d_send.at[i, direction, step],
+            d_recv.at[i, direction, step],
+            right if direction == 0 else left,
+        )
+
+    def to_sibling(i, slot):
+        offset = 0 if slot == 0 else (-slot if slot < pairs else slot - pairs + 1)
+        source = d_in[i] if slot == 0 else block(i, offset)
+        return remote(source, block(i, offset), s_send.at[i, slot], s_recv.at[i, slot], sibling)
+
+    def from_sibling(i, slot):
+        offset = 0 if slot == 0 else (-slot if slot < pairs else slot - pairs + 1)
+        here = d_out[i].at[(spot + offset) * 2 + 1 - core]
+        return remote(here, here, s_send.at[i, slot], s_recv.at[i, slot], sibling)
+
+    def from_side(i, direction, step):
+        here = block(i, -step if direction == 0 else step)
+        return remote(
+            here,
+            here,
+            d_send.at[i, direction, step - 1],
+            d_recv.at[i, direction, step - 1],
+            sibling,
+        )
+
+    if n == 4:
+        _, by_x, by_y, _ = peers
+        dev_x, dev_y = {"tensor": by_x}, {"tensor": by_y}
+
+    def halves(ref):
+        rows = ref.shape[0] // 2
+        return ref.at[pl.ds(0, rows)], ref.at[pl.ds(rows, rows)]
+
+    def t_copy(i, which):
+        slot, half, device, source = (
+            (me, 0, dev_x, None),
+            (me, 1, dev_y, None),
+            (me, 1, dev_x, None),
+            (me, 0, dev_y, None),
+            (by_x, 0, dev_y, 1),
+            (by_y, 1, dev_x, 1),
+        )[which]
+        target = halves(t_out[i].at[slot])[half]
+        origin = halves(t_in[i])[half] if source is None else target
+        return remote(origin, target, t_send.at[i, which], t_recv.at[i, which], device)
+
+    def t_arrival(i, which):
+        slot, half = (
+            (by_x, 0),
+            (by_y, 1),
+            (by_x, 1),
+            (by_y, 0),
+            (peers[3], 0),
+            (peers[3], 1),
+        )[which]
+        here = halves(t_out[i].at[slot])[half]
+        return remote(here, here, t_send.at[i, which], t_recv.at[i, which], dev_x)
+
+    def t_direct(i, k, slot):
+        return remote(
+            t_in[i],
+            t_out[i].at[slot],
+            t_send.at[i, k],
+            t_recv.at[i, k],
+            {"tensor": lax.rem(me + k, n)},
+        )
+
+    for i in range(nt):
+        for k in range(4) if n == 4 else range(1, n):
+            (t_copy(i, k) if n == 4 else t_direct(i, k, me)).start()
+    for i in range(nd):
+        if pairs > 1:
+            pl.when(spot + 1 < pairs)(lambda i=i: to_side(i, 0, 0).start())
+            pl.when(spot >= 1)(lambda i=i: to_side(i, 1, 0).start())
+    for i in range(nd):
+        to_sibling(i, 0).start()
+    for i, source in enumerate(t_in + d_in):
+        pltpu.make_async_copy(source, stage[i], load_sem.at[i]).start()
+    for i, target in enumerate([t.at[me] for t in t_out] + [d.at[me_dp] for d in d_out]):
+        pltpu.make_async_copy((t_in + d_in)[i], stage[i], load_sem.at[i]).wait()
+        pltpu.make_async_copy(stage[i], target, store_sem.at[i]).start()
+
+    def dp_step(step):
+        for i in range(nd):
+
+            @pl.when(spot >= step)
+            def _(i=i):
+                from_side(i, 0, step).wait_recv()
+                if step < pairs - 1:
+                    pl.when(spot + 1 < pairs)(lambda: to_side(i, 0, step).start())
+                to_sibling(i, step).start()
+
+            @pl.when(spot + step < pairs)
+            def _(i=i):
+                from_side(i, 1, step).wait_recv()
+                if step < pairs - 1:
+                    pl.when(spot >= 1)(lambda: to_side(i, 1, step).start())
+                to_sibling(i, pairs - 1 + step).start()
+
+    if n == 4:
+        for i in range(nt):
+            t_arrival(i, 0).wait_recv()
+            t_copy(i, 4).start()
+            t_arrival(i, 1).wait_recv()
+            t_copy(i, 5).start()
+    for step in range(1, pairs):
+        dp_step(step)
+    for i in range(nt):
+        if n == 4:
+            for which in range(2, 6):
+                t_arrival(i, which).wait_recv()
+            for which in range(6):
+                t_copy(i, which).wait_send()
+        else:
+            for k in range(1, n):
+                t_direct(i, k, lax.rem(me + n - k, n)).wait_recv()
+            for k in range(1, n):
+                t_direct(i, k, me).wait_send()
+    for i in range(nd):
+        from_sibling(i, 0).wait_recv()
+        to_sibling(i, 0).wait_send()
+        for step in range(1, pairs):
+
+            @pl.when(spot >= step)
+            def _(i=i, step=step):
+                from_sibling(i, step).wait_recv()
+                to_sibling(i, step).wait_send()
+
+            @pl.when(spot + step < pairs)
+            def _(i=i, step=step):
+                from_sibling(i, pairs - 1 + step).wait_recv()
+                to_sibling(i, pairs - 1 + step).wait_send()
+
+        for step in range(pairs - 1):
+            pl.when((spot >= step) & (spot + 1 < pairs))(
+                lambda i=i, step=step: to_side(i, 0, step).wait_send()
+            )
+            pl.when((spot + step < pairs) & (spot >= 1))(
+                lambda i=i, step=step: to_side(i, 1, step).wait_send()
+            )
+    for i, target in enumerate([t.at[me] for t in t_out] + [d.at[me_dp] for d in d_out]):
+        pltpu.make_async_copy(stage[i], target, store_sem.at[i]).wait()
+
+
+def gather_all(tensor_arrays, dp_arrays, collective_id):
+    n, total = lax.axis_size("tensor"), lax.axis_size("dp")
+    nt, nd = len(tensor_arrays), len(dp_arrays)
+    pairs = total // 2
+    every = list(tensor_arrays) + list(dp_arrays)
+    lead = [n] * nt + [total] * nd
+    dma = pltpu.SemaphoreType.DMA
+    outs = pl.pallas_call(
+        functools.partial(gather_kernel, n, total, nt, nd),
+        out_shape=[
+            jax.ShapeDtypeStruct((count,) + a.shape, a.dtype) for count, a in zip(lead, every)
+        ],
+        in_specs=[ANY] * (nt + nd),
+        out_specs=[ANY] * (nt + nd),
+        scratch_shapes=[pltpu.VMEM(a.shape, a.dtype) for a in every]
+        + [
+            dma((nt + nd,)),
+            dma((nt + nd,)),
+            dma((nt, max(n, 6))),
+            dma((nt, max(n, 6))),
+            dma((nd, 2, pairs)),
+            dma((nd, 2, pairs)),
+            dma((nd, 2 * pairs)),
+            dma((nd, 2 * pairs)),
+        ],
+        compiler_params=pltpu.CompilerParams(
+            collective_id=collective_id, has_side_effects=True, vmem_limit_bytes=VMEM_BYTES
+        ),
+        name="gather_all",
+    )(*every)
+    return [o.reshape((o.shape[0] * o.shape[1],) + o.shape[2:]) for o in outs]
+
+
+def small_sum_kernel(n, in_ref, out_ref, slots, send_sem, recv_sem):
+    me = lax.axis_index("tensor")
+    greet([{"tensor": lax.rem(me + k, n)} for k in range(1, n)])
+
+    def copy(k, slot):
+        return remote(
+            in_ref,
+            slots.at[slot],
+            send_sem.at[k],
+            recv_sem.at[k],
+            {"tensor": lax.rem(me + k, n)},
+        )
+
+    for k in range(1, n):
+        copy(k, me).start()
+    slots[me] = in_ref[...]
+    for k in range(1, n):
+        copy(k, lax.rem(me + n - k, n)).wait_recv()
+    added = slots[0]
+    for j in range(1, n):
+        added = added + slots[j]
+    out_ref[...] = added
+    for k in range(1, n):
+        copy(k, me).wait_send()
+
+
+def small_sum(values, collective_id):
+    n = lax.axis_size("tensor")
+    flipped = values.T
+    summed = pl.pallas_call(
+        functools.partial(small_sum_kernel, n),
+        out_shape=jax.ShapeDtypeStruct(flipped.shape, flipped.dtype),
+        in_specs=[VMEM],
+        out_specs=VMEM,
+        scratch_shapes=[
+            pltpu.VMEM((n,) + flipped.shape, flipped.dtype),
+            pltpu.SemaphoreType.DMA((n,)),
+            pltpu.SemaphoreType.DMA((n,)),
+        ],
+        compiler_params=pltpu.CompilerParams(collective_id=collective_id, has_side_effects=True),
+        name="small_sum",
+    )(flipped)
+    return summed.T
+
+
+def scatter_kernel(n, total, nt, nd, *refs):
+    take = iter(refs)
+    t_in = [next(take) for _ in range(nt)]
+    d_in = [next(take) for _ in range(nd)]
+    t_out = [next(take) for _ in range(nt)]
+    d_out = [next(take) for _ in range(nd)]
+    t_own = [next(take) for _ in range(nt)]
+    t_mid = [next(take) for _ in range(nt)]
+    t_got = [next(take) for _ in range(nt)]
+    t_end = [next(take) for _ in range(nt)]
+    d_own = [next(take) for _ in range(nd)]
+    d_sib = [next(take) for _ in range(nd)]
+    d_side = [next(take) for _ in range(nd)]
+    t_load, d_load, t_send, t_recv, d_send, d_recv, s_send, s_recv = take
+    pairs = total // 2
+    me_dp = lax.axis_index("dp")
+    spot, core = lax.div(me_dp, 2), lax.rem(me_dp, 2)
+    sibling = {"dp": spot * 2 + 1 - core}
+    right, left = {"dp": (spot + 1) * 2 + core}, {"dp": (spot - 1) * 2 + core}
+    peers = tensor_peers(n)
+    me = peers[0]
+    f32 = jnp.float32
+
+    greet(tensor_devices(n) + dp_devices(total))
+
+    for i in range(nd):
+        remote(
+            d_in[i].at[:, 1 - core], d_sib[i], s_send.at[i], s_recv.at[i], sibling
+        ).start()
+    for i in range(nd):
+        pltpu.make_async_copy(d_in[i].at[:, core], d_own[i], d_load.at[i]).start()
+    if n == 4:
+        _, by_x, by_y, across = peers
+        dev_x, dev_y = {"tensor": by_x}, {"tensor": by_y}
+        width = t_in[0].shape[2] // 2
+        cut = (pl.ds(0, width), pl.ds(width, width))
+
+    def t_first(i, side, part):
+        slot = across if part == 0 else (by_x, by_y)[side]
+        return remote(
+            t_in[i].at[slot, :, cut[side]],
+            t_got[i].at[side, part],
+            t_send.at[i, side * 2 + part],
+            t_recv.at[i, side * 2 + part],
+            (dev_x, dev_y)[side],
+        )
+
+    def t_second(i, side):
+        return remote(
+            t_mid[i].at[side],
+            t_end[i].at[side],
+            t_send.at[i, 4 + side],
+            t_recv.at[i, 4 + side],
+            (dev_y, dev_x)[side],
+        )
+
+    def t_loads(i):
+        loads = [pltpu.make_async_copy(t_in[i].at[me], t_own[i], t_load.at[i, 0])]
+        if n == 4:
+            for side, slot in ((0, by_y), (1, by_x)):
+                loads.append(
+                    pltpu.make_async_copy(
+                        t_in[i].at[slot, :, cut[side]], t_mid[i].at[side], t_load.at[i, 1 + side]
+                    )
+                )
+        return loads
+
+    def t_direct(i, k, slot, landing):
+        return remote(
+            t_in[i].at[slot],
+            t_got[i].at[landing],
+            t_send.at[i, k],
+            t_recv.at[i, k],
+            {"tensor": lax.rem(me + k, n)},
+        )
+
+    for i in range(nt):
+        if n == 4:
+            for part in range(2):
+                for side in range(2):
+                    t_first(i, side, part).start()
+        else:
+            for k in range(1, n):
+                t_direct(i, k, lax.rem(me + k, n), me).start()
+        for load in t_loads(i):
+            load.start()
+
+    for i in range(nd):
+        pltpu.make_async_copy(d_in[i].at[:, core], d_own[i], d_load.at[i]).wait()
+        remote(
+            d_in[i].at[:, 1 - core], d_sib[i], s_send.at[i], s_recv.at[i], sibling
+        ).wait_recv()
+        for d in range(pairs):
+            d_own[i][d] = (d_own[i][d].astype(f32) + d_sib[i][d].astype(f32)).astype(
+                d_own[i].dtype
+            )
+
+    def d_copy(i, direction, slot, source):
+        return remote(
+            source,
+            d_side[i].at[direction, slot],
+            d_send.at[i, direction, slot],
+            d_recv.at[i, direction, slot],
+            (right, left)[direction],
+        )
+
+    def d_step(j):
+        for direction, d in ((0, pairs - 1 - j), (1, j)):
+            outer = spot == 0 if direction == 0 else spot == pairs - 1
+            inner = (
+                (spot > 0) & (spot < d) if direction == 0 else (spot < pairs - 1) & (spot > d)
+            )
+
+            @pl.when(outer)
+            def _(direction=direction, d=d):
+                for i in range(nd):
+                    d_copy(i, direction, j, d_own[i].at[d]).start()
+
+            @pl.when(inner)
+            def _(direction=direction, d=d):
+                for i in range(nd):
+                    here = d_side[i].at[direction, j]
+                    d_copy(i, direction, j, here).wait_recv()
+                    here[...] = (here[...].astype(f32) + d_own[i][d].astype(f32)).astype(
+                        here.dtype
+                    )
+                    d_copy(i, direction, j, here).start()
+
+    def t_forward(i):
+        loads = t_loads(i)
+        for side in range(2):
+            loads[1 + side].wait()
+            t_first(i, side, 0).wait_recv()
+            t_mid[i][side] = (
+                t_mid[i][side].astype(f32) + t_got[i][side, 0].astype(f32)
+            ).astype(t_mid[i].dtype)
+            t_second(i, side).start()
+
+    for j in range(max(pairs - 1, nt)):
+        if j < pairs - 1:
+            d_step(j)
+        if n == 4 and j < nt:
+            t_forward(j)
+
+    for i in range(nt):
+        t_loads(i)[0].wait()
+        if n == 4:
+            for side in range(2):
+                t_first(i, side, 1).wait_recv()
+                t_second(i, side).wait_recv()
+                t_out[i][:, cut[side]] = (
+                    t_own[i][:, cut[side]].astype(f32)
+                    + t_got[i][side, 1].astype(f32)
+                    + t_end[i][side].astype(f32)
+                ).astype(t_out[i].dtype)
+        else:
+            added = t_own[i][...].astype(f32)
+            for k in range(1, n):
+                source = lax.rem(me + n - k, n)
+                t_direct(i, k, me, source).wait_recv()
+                added = added + t_got[i][source].astype(f32)
+            t_out[i][...] = added.astype(t_out[i].dtype)
+
+    for i in range(nd):
+        d_out[i][...] = d_own[i][spot].astype(f32)
+
+        @pl.when(spot > 0)
+        def _(i=i):
+            slot = pairs - 1 - spot
+            here = d_side[i].at[0, slot]
+            d_copy(i, 0, slot, here).wait_recv()
+            d_out[i][...] = d_out[i][...] + here[...].astype(f32)
+
+        @pl.when(spot < pairs - 1)
+        def _(i=i):
+            here = d_side[i].at[1, spot]
+            d_copy(i, 1, spot, here).wait_recv()
+            d_out[i][...] = d_out[i][...] + here[...].astype(f32)
+
+    for i in range(nd):
+        remote(
+            d_in[i].at[:, 1 - core], d_sib[i], s_send.at[i], s_recv.at[i], sibling
+        ).wait_send()
+        for j in range(pairs - 1):
+            for direction, d in ((0, pairs - 1 - j), (1, j)):
+                pl.when(spot < d if direction == 0 else spot > d)(
+                    lambda i=i, direction=direction, j=j: d_copy(
+                        i, direction, j, d_side[i].at[direction, j]
+                    ).wait_send()
+                )
+    for i in range(nt):
+        if n == 4:
+            for side in range(2):
+                t_first(i, side, 0).wait_send()
+                t_first(i, side, 1).wait_send()
+                t_second(i, side).wait_send()
+        else:
+            for k in range(1, n):
+                t_direct(i, k, lax.rem(me + k, n), me).wait_send()
+
+
+def scatter_all(tensor_arrays, dp_arrays, collective_id):
+    n, total = lax.axis_size("tensor"), lax.axis_size("dp")
+    nt, nd = len(tensor_arrays), len(dp_arrays)
+    pairs = total // 2
+    shaped_t = [a.reshape(n, a.shape[0] // n, a.shape[1]) for a in tensor_arrays]
+    shaped_d = [a.reshape(pairs, 2, a.shape[0] // total, a.shape[1]) for a in dp_arrays]
+    dma = pltpu.SemaphoreType.DMA
+    own = [pltpu.VMEM(a.shape[1:], a.dtype) for a in shaped_t]
+    if n == 4:
+        halved = [(a.shape[1], a.shape[2] // 2) for a in shaped_t]
+        kind = [a.dtype for a in shaped_t]
+        mid = [pltpu.VMEM((2,) + h, k) for h, k in zip(halved, kind)]
+        got = [pltpu.VMEM((2, 2) + h, k) for h, k in zip(halved, kind)]
+        end = [pltpu.VMEM((2,) + h, k) for h, k in zip(halved, kind)]
+    else:
+        mid = [pltpu.VMEM((16, 128), a.dtype) for a in shaped_t]
+        got = [pltpu.VMEM(a.shape, a.dtype) for a in shaped_t]
+        end = [pltpu.VMEM((16, 128), a.dtype) for a in shaped_t]
+    outs = pl.pallas_call(
+        functools.partial(scatter_kernel, n, total, nt, nd),
+        out_shape=[jax.ShapeDtypeStruct(a.shape[1:], a.dtype) for a in shaped_t]
+        + [jax.ShapeDtypeStruct(a.shape[2:], jnp.float32) for a in shaped_d],
+        in_specs=[ANY] * (nt + nd),
+        out_specs=[VMEM] * (nt + nd),
+        scratch_shapes=own
+        + mid
+        + got
+        + end
+        + [pltpu.VMEM((pairs,) + a.shape[2:], a.dtype) for a in shaped_d]
+        + [pltpu.VMEM((pairs,) + a.shape[2:], a.dtype) for a in shaped_d]
+        + [pltpu.VMEM((2, max(pairs - 1, 1)) + a.shape[2:], a.dtype) for a in shaped_d]
+        + [
+            dma((nt, 3)),
+            dma((nd,)),
+            dma((nt, max(n, 6))),
+            dma((nt, max(n, 6))),
+            dma((nd, 2, pairs)),
+            dma((nd, 2, pairs)),
+            dma((nd,)),
+            dma((nd,)),
+        ],
+        compiler_params=pltpu.CompilerParams(
+            collective_id=collective_id, has_side_effects=True, vmem_limit_bytes=VMEM_BYTES
+        ),
+        name="scatter_all",
+    )(*shaped_t, *shaped_d)
+    return outs
 
 
 adapter_scale = 2.0
@@ -136,13 +688,20 @@
     rank_piece = output_up_factor.shape[1]
     query_columns = query_weight.shape[1]
     key_value_columns = key_value_weight.shape[2]
-    input_down_every, query_up_every, key_value_up_every, output_down_every, b_out_all = (
-        lax.all_gather(a_in, "dp", axis=0, tiled=True),
-        lax.all_gather(b_query, "dp", axis=0, tiled=True),
-        lax.all_gather(b_key_value, "dp", axis=0, tiled=True),
-        lax.all_gather(output_down_factor, "dp", axis=0, tiled=True),
-        lax.all_gather(output_up_factor, "dp", axis=0, tiled=True),
-    )
+    (
+        gathered,
+        input_down_every,
+        query_up_every,
+        key_value_up_every,
+        output_down_every,
+        b_out_all,
+    ) = gather_all(
+        [hidden_in],
+        [a_in, b_query, b_key_value, output_down_factor, output_up_factor],
+        0,
+    )
+    out_grad, gathered = lax.optimization_barrier((out_grad, gathered))
+    incoming_gradient = lax.all_gather(out_grad, "tensor", axis=0, tiled=True)
     adapter_overall_count = input_down_every.shape[0]
     position, adapter_hot, allowed = token_tables(
         seq_lengths[0], seq_adapter[0], tok_total, adapter_overall_count
@@ -166,7 +725,6 @@
         adapter_overall_count * adapter_rank_rows, query_columns
     )
     output_up_flattened = b_out_all.reshape(adapter_overall_count * rank_piece, full_width)
-    gathered = lax.all_gather(hidden_in, "tensor", axis=0, tiled=True)
     col_start = own_slot * narrow_cast
     local_columns = lax.dynamic_slice_in_dim(gathered, col_start, narrow_cast, 1)
     rank_partial_sum = choose_rank_rows(
@@ -174,7 +732,7 @@
         contract_trailing_axis(local_columns, input_down_flattened),
         3 * adapter_rank_rows,
     )
-    input_rank_rows = lax.psum(rank_partial_sum, "tensor").astype(jnp.bfloat16)
+    input_rank_rows = small_sum(rank_partial_sum, 1).astype(jnp.bfloat16)
     adapter_query_delta = expand_from_rank(onehot_halfprec, input_rank_rows[:, :adapter_rank_rows])
     adapter_key_delta = expand_from_rank(
         onehot_halfprec, input_rank_rows[:, adapter_rank_rows : 2 * adapter_rank_rows]
@@ -216,7 +774,25 @@
         contract_trailing_axis(blended_output, output_down_flattened),
         adapter_rank_rows,
     )
-    output_rank_rows = lax.psum(output_partial_sum, "tensor").astype(jnp.bfloat16)
+    grad_part = (
+        adapter_scale
+        * choose_rank_rows(
+            onehot_single,
+            contract_trailing_axis(incoming_gradient, output_up_flattened),
+            rank_piece,
+        )
+    ).astype(jnp.bfloat16)
+    placed_part = lax.dynamic_update_slice_in_dim(
+        jnp.zeros((tok_total, adapter_rank_rows), jnp.float32),
+        grad_part.astype(jnp.float32),
+        own_slot * rank_piece,
+        1,
+    )
+    both_ranks = small_sum(jnp.concatenate([output_partial_sum, placed_part], axis=1), 2).astype(
+        jnp.bfloat16
+    )
+    output_rank_rows = both_ranks[:, :adapter_rank_rows]
+    output_rank_gradient = both_ranks[:, adapter_rank_rows:]
     adapter_output_delta = expand_from_rank(
         onehot_halfprec,
         lax.dynamic_slice_in_dim(output_rank_rows, own_slot * rank_piece, rank_piece, 1),
@@ -232,16 +808,6 @@
         scatter_dimension=0,
         tiled=True,
     )
-    incoming_gradient = lax.all_gather(out_grad, "tensor", axis=0, tiled=True)
-    grad_part = (
-        adapter_scale
-        * choose_rank_rows(
-            onehot_single,
-            contract_trailing_axis(incoming_gradient, output_up_flattened),
-            rank_piece,
-        )
-    ).astype(jnp.bfloat16)
-    output_rank_gradient = lax.all_gather(grad_part, "tensor", axis=1, tiled=True)
     output_up_gradient = (
         adapter_scale * contract_leading_axis(adapter_output_delta, incoming_gradient)
     ).reshape(adapter_overall_count, rank_piece, full_width)
@@ -289,7 +855,7 @@
         ],
         axis=1,
     )
-    input_rank_gradient = (adapter_scale * lax.psum(backward_partial_sum, "tensor")).astype(
+    input_rank_gradient = (adapter_scale * small_sum(backward_partial_sum, 3)).astype(
         jnp.bfloat16
     )
     query_up_gradient = (
@@ -320,16 +886,25 @@
         col_start,
         1,
     )
-    input_grad = lax.psum_scatter(
-        (heads_sum + placed).astype(jnp.bfloat16), "tensor", scatter_dimension=0, tiled=True
-    )
-    summed_a_in, summed_b_query, summed_b_kv, summed_a_out, summed_b_out = (
-        lax.psum_scatter(input_down_gradient, "dp", scatter_dimension=0, tiled=True),
-        lax.psum_scatter(query_up_gradient, "dp", scatter_dimension=0, tiled=True),
-        lax.psum_scatter(grad_b_kv, "dp", scatter_dimension=0, tiled=True),
-        lax.psum_scatter(output_down_gradient, "dp", scatter_dimension=0, tiled=True),
-        lax.psum_scatter(output_up_gradient, "dp", scatter_dimension=0, tiled=True),
-    )
+    half = jnp.bfloat16
+    wide = lambda grad: grad.reshape(-1, grad.shape[-1]).astype(half)
+    input_grad, *summed = scatter_all(
+        [(heads_sum + placed).astype(half)],
+        [
+            wide(input_down_gradient),
+            wide(query_up_gradient),
+            wide(grad_b_kv),
+            wide(output_down_gradient),
+            wide(output_up_gradient),
+        ],
+        4,
+    )
+    summed_a_in, summed_b_query, summed_b_kv, summed_a_out, summed_b_out = [
+        s.reshape(factor.shape)
+        for s, factor in zip(
+            summed, (a_in, b_query, b_key_value, output_down_factor, output_up_factor)
+        )
+    ]
     return (
         attn_out,
         input_grad,

time: 622 us -> 310 us (0.50)
  waiting for transfers between devices: 380 us -> 1.64 us
  Pallas kernels: 0 us -> 138 us
  blocking collectives: 73.8 us -> 0 us
  matrix products: 117 us -> 127 us
    reduce_scatter x4 -> x0, waiting for transfers between devices: 189 us -> none  [the longest x1 71.8 us: local(): lax.psum_scatter(input_down_gradient, 'dp', scatter_dimension=0, tiled=True)]
    pallas_call x0 -> x5, Pallas kernels: none -> 138 us  [the longest x1 70.5 us: scatter_all(): pl.pallas_call(functools.partial(scatter_kernel, n, total, nt, nd), out_s...]
    all_gather x3 -> x0, waiting for transfers between devices: 83.4 us -> none  [the longest x1 53.1 us: local(): gathered = lax.all_gather(hidden_in, 'tensor', axis=0, tiled=True)]
    reduce_scatter x1, waiting for transfers between devices: 58.7 us -> 0.01 us  [local(): lax.psum_scatter((jnp.dot(blended_output, output_weight, preferred_elemen...]
    all_gather x4 -> x0, blocking collectives: 49.9 us -> none  [the longest x1 15.1 us: local(): lax.all_gather(output_down_factor, 'dp', axis=0, tiled=True)]
    all_gather x1, waiting for transfers between devices: 28.8 us -> 1.6 us  [local(): incoming_gradient = lax.all_gather(out_grad, 'tensor', axis=0, tiled=True)]
    psum x2 -> x0, blocking collectives: 23.9 us -> none  [the longest x1 12 us: local(): lax.psum(output_partial_sum, 'tensor').astype(jnp.bfloat16)]
    unnamed x11 -> x2, waiting for transfers between devices: 20.4 us -> 0.03 us
  transfers between devices with their start and end apart: 10 -> 2, of which waited for: 9 -> 1; matrix products, arithmetic and copies ran while one was open for 11% -> 43% of each run, Pallas kernels for 0% -> 28%
where the time goes in v1:
time: 310 us; the launch traced here: 305 us
  Pallas kernels  138 us (45%)
  matrix products  127 us (41%)
  between operations  14.8 us (5%)
  local copies, waits for them, and re-layouts  12.5 us (4%)
  other arithmetic  11.5 us (4%)
    pallas_call x1, Pallas kernels, scatter_all(): pl.pallas_call(functools.partial(scatter_kernel, n, total, nt, nd), out_s...  70.5 us
    dot_general x10, matrix products, contract_trailing_axis(): lax.dot_general(left, right, (((1,), (1,)), ((), ())), preferred_element_...  59 us
    pallas_call x1, Pallas kernels, gather_all(): pl.pallas_call(functools.partial(gather_kernel, n, total, nt, nd), out_sh...  46.9 us
    pallas_call x3, Pallas kernels, small_sum(): pl.pallas_call(functools.partial(small_sum_kernel, n), out_shape=jax.Shap...  20.2 us
    dot_general x1, matrix products, local(): jnp.dot(blended_output, output_weight, preferred_element_type=jnp.float32)  13 us
    dot_general x1, matrix products, local(): jnp.dot(gathered, query_weight, preferred_element_type=jnp.float32)  9.63 us
    dot_general x6, matrix products, contract_leading_axis(): lax.dot_general(left, right, (((0,), (0,)), ((), ())), preferred_element_...  8.4 us
    unnamed x53, local copies, waits for them, and re-layouts  7.84 us
  transfers between devices with their start and end apart: 2, of which 1 were waited for; matrix products, arithmetic and copies ran while one was open for 43% of the time, Pallas kernels for 28%

profile of v1, /device:TPU:23, one launch (start us, length us, event | category | flops | bytes accessed | tf_op | source)
XLA Modules:
  0.0 304.8 jit_solution(18244659546784887396)
XLA Ops:
  7.2 46.9 %gather_all.1 = (bf16[4,64,8192]{2,1,0:T(8,128)(2,1)}, bf16[8,2,48,2048]{3,2,1,0:T(8,128)(2,1)}, bf16[8,2,16,1024]{3,2,1,0:T(8,128)(2,1)}, bf16[8,2,2,16,256]{4,...) custom-call(bf16[64,8192]{1,0:T(8,128)(2,1)} %refs_0_.1, ...), custom_call_target="tpu_custom_call" | custom-call | tf_op jit(solution)/shard_map/gather_all/pallas_call | solution.py:240
  54.3 0.9 reduce-window.4
  55.1 0.7 fusion.75
  55.8 0.7 select_reduce_fusion
  56.6 3.9 %fusion.24 = f32[256,48]{0,1:T(8,128)} fusion(bf16[16,48,2048]{2,1,0:T(8,128)(2,1)} %bitcast.234, bf16[256,8192]{1,0:T(8,128)(2,1)} %bitcast.279, s32[]{:T(128)S(6)} %select_n.12, f32[256,16]{0,1:T(8,128)S(1)} %get-tuple-element.63), kind=kOutput, calls=%fused_computation.41 | convolution fusion | flops 805687296 | bytes 4259844 | tf_op jit(solution)/shard_map/dot_general | solution.py:567
  60.4 5.9 %small_sum.3 = f32[48,256]{1,0:T(8,128)} custom-call(f32[48,256]{1,0:T(8,128)} %bitcast.287), custom_call_target="tpu_custom_call" | custom-call | tf_op jit(solution)/shard_map/small_sum/pallas_call | solution.py:295
  66.3 0.8 convert_bitcast_fusion
  67.2 0.3 convolution_multiply_fusion.3
  67.5 9.6 %convolution_add_fusion.4 = f32[256,1024]{1,0:T(8,128)S(1)} fusion(f32[256,1024]{1,0:T(8,128)S(1)} %convolution_multiply_fusion.3, bf16[256,8192]{1,0:T(8,128)(2,1)} %bitcast.280, bf16[8192,1024]{1,0:T(8,128)(2,1)} %param.16), kind=kOutput, calls=%fused_computation.33 | convolution fusion | flops 4295229440 | bytes 23068672 | tf_op jit(solution)/shard_map/dot_general | solution.py:743
  77.1 0.3 copy.141
  77.5 1.3 reshape_reshape.13
  78.9 0.3 multiply_cosine_fusion
  79.2 0.7 fusion.62
  80.0 5.3 %fusion.8 = f32[256,256]{0,1:T(8,128)S(1)} fusion(bf16[256,8192]{1,0:T(8,128)(2,1)} %bitcast.281, bf16[2,8192,256]{2,1,0:T(8,128)(2,1)} %param.17), kind=kOutput, calls=%fused_computation.12 | convolution fusion | flops 1073741824 | bytes 8650752 | tf_op jit(solution)/shard_map/dot_general | solution.py:748
  85.3 0.2 fusion.25
  85.6 4.1 %fusion.11 = f32[256,256]{0,1:T(8,128)S(1)} fusion(bf16[256,8192]{1,0:T(8,128)(2,1)S(1)} %bitcast.283, bf16[2,8192,256]{2,1,0:T(8,128)(2,1)} %param.17), kind=kOutput, calls=%fused_computation.15 | convolution fusion | flops 1073741824 | bytes 8650752 | tf_op jit(solution)/shard_map/dot_general | solution.py:753
  89.7 0.2 fusion.27
  90.1 1.0 fusion.42
  91.1 3.3 %fusion.87 = (f32[2,4,256]{2,1,0:T(4,128)S(1)}, f32[2,4,256,256]{2,3,1,0:T(8,128)}) fusion(pred[256,256]{0,1:T(8,128)(4,1)} %fusion.62, bf16[256,2,128,1]{0,2,3,1:T(8,128)(2,1)S(1)} %fusion.65, bf16[256,2,4,128]{0,3,2,1:T(8,128)(2,1)} %fusion.42), kind=kOutput, calls=%fused_computation.150 | convolution fusion | flops 136315136 | bytes 2826240 | tf_op jit(solution)/shard_map/sub | solution.py:631
  94.3 2.0 convolution_convert_fusion.2
  96.3 0.3 fusion.31
  96.7 13.0 %fusion.88 = f32[256,8192]{1,0:T(8,128)} fusion(bf16[256,1024]{0,1:T(8,128)(2,1)S(1)} %bitcast.237, bf16[1024,8192]{1,0:T(8,128)(2,1)} %param.18), kind=kOutput, calls=%fused_computation.151 | convolution fusion | flops 4294967296 | bytes 25690112 | tf_op jit(solution)/shard_map/dot_general | solution.py:803
  109.7 1.6 all-gather.2.cloned.1.call-done
  111.3 3.6 %fusion.38 = f32[256,4]{0,1:T(4,128)S(1)} fusion(bf16[256,8192]{1,0:T(8,128)(2,1)} %all-gather.2.cloned.1.call-done, bf16[16,4,8192]{2,1,0:T(4,128)(2,1)S(1)} %bitcast.261, f32[256,16]{0,1:T(8,128)S(1)} %copy-done.22), kind=kOutput, calls=%fused_computation.63 | convolution fusion | flops 268467200 | bytes 5263360 | tf_op jit(solution)/shard_map/dot_general | solution.py:567
  115.0 0.6 maximum_bitcast_fusion.1.in_ref
  115.6 5.5 %small_sum.4 = f32[32,256]{1,0:T(8,128)} custom-call(f32[32,256]{1,0:T(8,128)} %maximum_bitcast_fusion.1.in_ref), custom_call_target="tpu_custom_call" | custom-call | tf_op jit(solution)/shard_map/small_sum/pallas_call | solution.py:295
  121.1 0.8 convert_bitcast_fusion.1
  121.9 6.6 %fusion.3 = bf16[256,8192]{1,0:T(8,128)(2,1)} fusion(f32[256,8192]{1,0:T(8,128)} %fusion.88, bf16[256,64]{0,1:T(8,128)(2,1)S(1)} %mul.435, bf16[64,8192]{1,0:T(8,128)(2,1)S(1)} %reshape_reshape.13), kind=kOutput, calls=%fused_computation.6 | convolution fusion | flops 274726912 | bytes 13664256 | tf_op jit(solution)/shard_map/dot_general | solution.py:805
  128.6 1.0 copy-done.6
  129.6 0.3 fusion.89
  129.9 11.6 %fusion.23 = bf16[256,1024]{1,0:T(8,128)(2,1)S(1)} fusion(f32[256,1024]{1,0:T(8,128)S(1)} %fusion.89, bf16[256,8192]{1,0:T(8,128)(2,1)} %all-gather.2.cloned.1.call-done, bf16[1024,8192]{1,0:T(8,128)(2,1)} %param.18), kind=kOutput, calls=%fused_computation.40 | convolution fusion | flops 4295491584 | bytes 22544384 | tf_op jit(solution)/shard_map/dot_general | solution.py:567
  141.5 0.2 copy.150
  141.7 2.1 fusion.30
  143.9 0.2 fusion.29
  144.2 1.8 fusion.90
  146.0 4.5 %convolution_bitcast_fusion.1 = f32[256,2,128]{0,2,1:T(8,128)S(1)} fusion(bf16[256,2,4,128]{0,3,2,1:T(8,128)(2,1)S(1)} %copy-done.7, f32[2,256,256,4]{2,1,3,0:T(8,128)} %fusion.90, f32[2,4,256,256]{2,3,1,0:T(8,128)} %get-tuple-element.65, f32[2,4,256]{2,1,0:T(4,128)S(1)} %get-tuple-element.64), kind=kOutput, calls=%fused_computation.53 | convolution fusion | flops 137890048 | bytes 4988928 | tf_op jit(solution)/shard_map/gpts,tgpe->sge/dot_general | solution.py:661
  150.7 0.2 fusion.28
  151.0 0.7 copy.121
  151.8 4.5 %fusion.52 = f32[2,128,4,256]{3,1,2,0:T(8,128)S(1)} fusion(bf16[256,2,128,1]{0,2,3,1:T(8,128)(2,1)S(1)} %copy-done.16, f32[2,256,256,4]{2,1,3,0:T(8,128)} %fusion.90, f32[2,4,256,256]{2,3,1,0:T(8,128)} %get-tuple-element.65, f32[2,4,256]{2,1,0:T(4,128)S(1)} %get-tuple-element.64), kind=kOutput, calls=%fused_computation.80 | convolution fusion | flops 137890048 | bytes 5382144 | tf_op jit(solution)/shard_map/gpts,sge->tgpe/dot_general | solution.py:658
  156.4 0.2 pad_maximum_fusion
  156.8 0.5 copy-done.13
  157.2 0.2 fusion.34
  157.4 0.2 fusion.33
  157.7 0.2 fusion.46
  157.9 0.3 fusion.32
  158.2 0.6 maximum_bitcast_fusion.in_ref
  158.8 8.9 %small_sum.5 = f32[48,256]{1,0:T(8,128)} custom-call(f32[48,256]{1,0:T(8,128)} %maximum_bitcast_fusion.in_ref), custom_call_target="tpu_custom_call" | custom-call | tf_op jit(solution)/shard_map/small_sum/pallas_call | solution.py:295
  167.7 0.8 fusion.68
  168.5 29.2 %fusion.91 = f32[256,8192]{1,0:T(8,128)} fusion(bf16[256,1024]{0,1:T(8,128)(2,1)S(1)} %fusion.44, bf16[8192,1024]{1,0:T(8,128)(2,1)} %param.16), kind=kOutput, calls=%fused_computation.154 | convolution fusion | flops 4294967296 | bytes 25690112 | tf_op jit(solution)/shard_map/dot_general | solution.py:567
  197.7 6.0 %convolution_add_fusion.1 = f32[256,8192]{1,0:T(8,128)S(1)} fusion(f32[256,8192]{1,0:T(8,128)} %fusion.91, bf16[256,256]{0,1:T(8,128)(2,1)S(1)} %bitcast.251, bf16[2,8192,256]{2,1,0:T(8,128)(2,1)} %param.17), kind=kOutput, calls=%fused_computation.3 | convolution fusion | flops 1075838976 | bytes 21102592 | tf_op jit(solution)/shard_map/dot_general | solution.py:567
  203.7 3.8 %convolution_add_fusion = f32[256,8192]{1,0:T(8,128)S(1)} fusion(f32[256,8192]{1,0:T(8,128)S(1)} %convolution_add_fusion.1, bf16[256,256]{0,1:T(8,128)(2,1)S(1)} %bitcast.265, bf16[2,8192,256]{2,1,0:T(8,128)(2,1)} %param.17), kind=kOutput, calls=%fused_computation.2 | convolution fusion | flops 1075838976 | bytes 21102592 | tf_op jit(solution)/shard_map/dot_general | solution.py:567
  207.5 1.2 fusion.17
  208.7 2.5 convert_element_type.161
  211.2 1.1 convolution_convert_fusion.1
  212.3 1.1 fusion.22
  213.5 3.9 %convolution_convert_fusion = bf16[768,2048]{1,0:T(8,128)(2,1)} fusion(bf16[256,768]{0,1:T(8,128)(2,1)S(1)} %bitcast.231, bf16[256,8192]{1,0:T(8,128)(2,1)} %bitcast.282, s32[]{:T(128)S(6)} %select_n.12), kind=kOutput, calls=%fused_computation.21 | convolution fusion | flops 806879232 | bytes 4587524 | tf_op jit(solution)/shard_map/dot_general | solution.py:573
  217.4 1.8 fusion.4
  219.2 70.5 %scatter_all.1 = (bf16[64,8192]{1,0:T(8,128)(2,1)}, f32[96,2048]{1,0:T(8,128)}, f32[32,1024]{1,0:T(8,128)}, f32[64,256]{1,0:T(8,128)}, f32[32,1024]{1,0:T(8,128)}, /*index=5*/f32[8,8192]{1,0:T(8,128)}) custom-call(bf16[4,64,8192]{2,1,0:T(8,128)(2,1)} %bitcast.226, bf16[4,2,96,2048]{3,2,1,0:T(8,128)(2,1)} %bitcast.225, bf16[4,2,32,1024]{3,2,1,0:T(8,128)(2,1)} %bitcast.242, ...), custom_call_target="tpu_custom_call" | custom-call | tf_op jit(solution)/shard_map/scatter_all/pallas_call | solution.py:530
  289.7 1.8 reshape.381
  291.5 2.3 copy.160
  293.7 2.1 copy.161
  295.8 0.7 copy.162
  296.4 0.6 copy.163
  297.1 0.7 copy.164
  (76 shorter events, 1.2 us)
Async XLA Ops:
  7.2 104.1 %all-gather.2.cloned.1.call-start = ((), (), s32[]{:S(2)}) async-start(), calls=%async_computation.1 | async-start | bytes 5242880 | tf_op jit(solution)/shard_map/all_gather | solution.py:704
  54.2 13.0 %copy-start.3 = (bf16[8,2,16,1024]{3,2,1,0:T(8,128)(2,1)S(1)}, bf16[8,2,16,1024]{3,2,1,0:T(8,128)(2,1)}, u32[]{:S(2)}) copy-start(bf16[8,2,16,1024]{3,2,1,0:T(8,128)(2,1)} %get-tuple-element.25) | copy-start | bytes 1572868
  54.2 237.3 %reduce-scatter.2.cloned.1.call-start = ((), (), s32[]{:S(2)}) async-start(), calls=%async_computation.2 | async-start | bytes 5242880 | tf_op jit(solution)/shard_map/reduce_scatter | solution.py:801
  56.5 3.9 %copy-start.20 = (f32[256,16]{0,1:T(8,128)}, f32[256,16]{0,1:T(8,128)S(1)}, u32[]{:S(2)}) copy-start(f32[256,16]{0,1:T(8,128)S(1)} %get-tuple-element.63) | copy-start | bytes 49156
  77.1 2.8 copy-start.12
  80.0 5.6 %copy-start.14 = (bf16[4,64,8192]{2,1,0:T(8,128)(2,1)S(1)}, bf16[4,64,8192]{2,1,0:T(8,128)(2,1)}, u32[]{:S(2)}) copy-start(bf16[4,64,8192]{2,1,0:T(8,128)(2,1)} %get-tuple-element.21) | copy-start | bytes 12582916
  89.9 4.4 %copy-start.8 = (bf16[256,256]{0,1:T(8,128)(2,1)}, bf16[256,256]{0,1:T(8,128)(2,1)S(1)}, u32[]{:S(2)}) copy-start(bf16[256,256]{0,1:T(8,128)(2,1)S(1)} %fusion.27) | copy-start | bytes 393220
  90.0 4.3 %copy-start.15 = (bf16[256,2,128,1]{0,2,3,1:T(8,128)(2,1)}, bf16[256,2,128,1]{0,2,3,1:T(8,128)(2,1)S(1)}, u32[]{:S(2)}) copy-start(bf16[256,2,128,1]{0,2,3,1:T(8,128)(2,1)S(1)} %fusion.65) | copy-start | bytes 393220
  94.3 2.0 copy-start.5
  94.3 2.0 copy-start.21
  96.7 14.7 %copy-start.2 = (bf16[8,2,4,8192]{3,2,1,0:T(4,128)(2,1)S(1)}, bf16[8,2,4,8192]{3,2,1,0:T(4,128)(2,1)}, u32[]{:S(2)}) copy-start(bf16[8,2,4,8192]{3,2,1,0:T(4,128)(2,1)} %get-tuple-element.28) | copy-start | bytes 3145732
  96.7 14.7 %copy-start.22 = (f32[256,16]{0,1:T(8,128)S(1)}, f32[256,16]{0,1:T(8,128)}, u32[]{:S(2)}) copy-start(f32[256,16]{0,1:T(8,128)} %copy-done.20) | copy-start | bytes 49156
  121.9 6.7 %copy-start.10 = (bf16[256,64]{0,1:T(8,128)(2,1)}, bf16[256,64]{0,1:T(8,128)(2,1)S(1)}, u32[]{:S(2)}) copy-start(bf16[256,64]{0,1:T(8,128)(2,1)S(1)} %mul.435) | copy-start | bytes 98308
  128.5 1.0 copy-start.6
  141.7 2.5 copy-start.9
  141.7 4.3 %copy-start.7 = (bf16[256,2,4,128]{0,3,2,1:T(8,128)(2,1)S(1)}, bf16[256,2,4,128]{0,3,2,1:T(8,128)(2,1)}, u32[]{:S(2)}) copy-start(bf16[256,2,4,128]{0,3,2,1:T(8,128)(2,1)} %fusion.42) | copy-start | bytes 1572868
  146.0 5.7 %copy-start.16 = (bf16[256,2,128,1]{0,2,3,1:T(8,128)(2,1)S(1)}, bf16[256,2,128,1]{0,2,3,1:T(8,128)(2,1)}, u32[]{:S(2)}) copy-start(bf16[256,2,128,1]{0,2,3,1:T(8,128)(2,1)} %copy-done.15) | copy-start | bytes 393220
  156.3 1.0 copy-start.13
  156.3 1.0 copy-start.23
  156.6 1.3 copy-start.4
  203.7 3.8 %copy-start.1 = (bf16[8,2,48,2048]{3,2,1,0:T(8,128)(2,1)S(1)}, bf16[8,2,48,2048]{3,2,1,0:T(8,128)(2,1)}, u32[]{:S(2)}) copy-start(bf16[8,2,48,2048]{3,2,1,0:T(8,128)(2,1)} %get-tuple-element.23) | copy-start | bytes 9437188
  211.2 6.2 %copy-start = (bf16[256,8192]{1,0:T(8,128)(2,1)S(1)}, bf16[256,8192]{1,0:T(8,128)(2,1)}, u32[]{:S(2)}) copy-start(bf16[256,8192]{1,0:T(8,128)(2,1)} %all-gather.2.cloned.1.call-done) | copy-start | bytes 12582916
  211.2 6.2 %copy-start.11 = (bf16[256,64]{0,1:T(8,128)(2,1)S(1)}, bf16[256,64]{0,1:T(8,128)(2,1)}, u32[]{:S(2)}) copy-start(bf16[256,64]{0,1:T(8,128)(2,1)} %copy-done.10) | copy-start | bytes 98308
  289.6 6.1 %copy-start.18 = (f32[32,1024]{1,0:T(8,128)S(1)}, f32[32,1024]{1,0:T(8,128)}, u32[]{:S(2)}) copy-start(f32[32,1024]{1,0:T(8,128)} %get-tuple-element.31) | copy-start | bytes 393220
  289.7 6.8 %copy-start.19 = (f32[64,256]{1,0:T(8,128)S(1)}, f32[64,256]{1,0:T(8,128)}, u32[]{:S(2)}) copy-start(f32[64,256]{1,0:T(8,128)} %get-tuple-element.32) | copy-start | bytes 196612
  289.7 7.4 %copy-start.17 = (f32[32,1024]{1,0:T(8,128)S(1)}, f32[32,1024]{1,0:T(8,128)}, u32[]{:S(2)}) copy-start(f32[32,1024]{1,0:T(8,128)} %get-tuple-element.33) | copy-start | bytes 393220
Sparse Core Ops, SparseCore 0:
  54.3 56.9 all-gather.1
  128.7 60.7 reduce-scatter.1

commit v2 on v1

--- a/solution.py
+++ b/solution.py
@@ -308,20 +308,17 @@
     return summed.T
 
 
-def scatter_kernel(n, total, nt, nd, *refs):
+def finish_kernel(n, total, tile, nd, *refs):
     take = iter(refs)
-    t_in = [next(take) for _ in range(nt)]
+    rows_ref, adapter_ref, down_ref, query_w, key_value_w = [next(take) for _ in range(5)]
     d_in = [next(take) for _ in range(nd)]
-    t_out = [next(take) for _ in range(nt)]
+    t_out = next(take)
     d_out = [next(take) for _ in range(nd)]
-    t_own = [next(take) for _ in range(nt)]
-    t_mid = [next(take) for _ in range(nt)]
-    t_got = [next(take) for _ in range(nt)]
-    t_end = [next(take) for _ in range(nt)]
+    part, added, got, end, query_buf, key_value_buf = [next(take) for _ in range(6)]
     d_own = [next(take) for _ in range(nd)]
     d_sib = [next(take) for _ in range(nd)]
     d_side = [next(take) for _ in range(nd)]
-    t_load, d_load, t_send, t_recv, d_send, d_recv, s_send, s_recv = take
+    w_sem, d_load, t_send, t_recv, d_send, d_recv, s_send, s_recv = take
     pairs = total // 2
     me_dp = lax.axis_index("dp")
     spot, core = lax.div(me_dp, 2), lax.rem(me_dp, 2)
@@ -330,76 +327,117 @@
     peers = tensor_peers(n)
     me = peers[0]
     f32 = jnp.float32
-
-    greet(tensor_devices(n) + dp_devices(total))
-
-    for i in range(nd):
-        remote(
-            d_in[i].at[:, 1 - core], d_sib[i], s_send.at[i], s_recv.at[i], sibling
-        ).start()
-    for i in range(nd):
-        pltpu.make_async_copy(d_in[i].at[:, core], d_own[i], d_load.at[i]).start()
+    rows, width = t_out.shape
+    half = width // 2
+    block = width // n
+    steps = half // tile
+    query_columns = query_w.shape[1]
+    key_value_columns = key_value_w.shape[2]
     if n == 4:
         _, by_x, by_y, across = peers
         dev_x, dev_y = {"tensor": by_x}, {"tensor": by_y}
-        width = t_in[0].shape[2] // 2
-        cut = (pl.ds(0, width), pl.ds(width, width))
-
-    def t_first(i, side, part):
-        slot = across if part == 0 else (by_x, by_y)[side]
+
+    def column(step, side):
+        return pl.multiple_of(side * half + step * tile, tile)
+
+    def loads(step, side):
+        span = pl.ds(column(step, side), tile)
+        return (
+            pltpu.make_async_copy(query_w.at[span, :], query_buf.at[side], w_sem.at[side, 0]),
+            pltpu.make_async_copy(
+                key_value_w.at[:, span, :], key_value_buf.at[side], w_sem.at[side, 1]
+            ),
+        )
+
+    for side in range(2):
+        for load in loads(0, side):
+            load.start()
+
+    greet(tensor_devices(n) + dp_devices(total))
+
+    def d_pair(i):
+        return remote(d_in[i].at[:, 1 - core], d_sib[i], s_send.at[i], s_recv.at[i], sibling)
+
+    for i in range(nd):
+        d_pair(i).start()
+    for i in range(nd):
+        pltpu.make_async_copy(d_in[i].at[:, core], d_own[i], d_load.at[i]).start()
+
+    def span_of(slot):
+        return pl.ds(pl.multiple_of(slot * rows, rows), rows)
+
+    def t_first(step, side, which):
+        slot = across if which == 0 else (by_x, by_y)[side]
         return remote(
-            t_in[i].at[slot, :, cut[side]],
-            t_got[i].at[side, part],
-            t_send.at[i, side * 2 + part],
-            t_recv.at[i, side * 2 + part],
+            part.at[span_of(slot), pl.ds(column(step, side), tile)],
+            got.at[side, which, :, pl.ds(pl.multiple_of(step * tile, tile), tile)],
+            t_send.at[side * 2 + which, step],
+            t_recv.at[side * 2 + which, step],
             (dev_x, dev_y)[side],
         )
 
-    def t_second(i, side):
+    def t_second(step, side):
+        span = pl.ds(pl.multiple_of(step * tile, tile), tile)
         return remote(
-            t_mid[i].at[side],
-            t_end[i].at[side],
-            t_send.at[i, 4 + side],
-            t_recv.at[i, 4 + side],
+            got.at[side, 0, :, span],
+            end.at[side, :, span],
+            t_send.at[4 + side, step],
+            t_recv.at[4 + side, step],
             (dev_y, dev_x)[side],
         )
 
-    def t_loads(i):
-        loads = [pltpu.make_async_copy(t_in[i].at[me], t_own[i], t_load.at[i, 0])]
+    def t_direct(step, side, k, slot, landing):
+        span = pl.ds(column(step, side), tile)
+        return remote(
+            part.at[span_of(slot), span],
+            got.at[landing, :, span],
+            t_send.at[side * n + k, step],
+            t_recv.at[side * n + k, step],
+            {"tensor": lax.rem(me + k, n)},
+        )
+
+    def compute(step, side):
+        for load in loads(step, side):
+            load.wait()
+        first = column(step, side)
+        added[...] = (
+            contract_trailing_axis(rows_ref[:, :query_columns], query_buf[side])
+            + contract_trailing_axis(
+                rows_ref[:, query_columns : query_columns + key_value_columns],
+                key_value_buf[side, 0],
+            )
+            + contract_trailing_axis(
+                rows_ref[:, query_columns + key_value_columns :], key_value_buf[side, 1]
+            )
+        )
+
+        @pl.when(lax.div(first, block) == me)
+        def _():
+            local_column = pl.multiple_of(first - me * block, tile)
+            added[...] += jnp.dot(
+                adapter_ref[...],
+                down_ref[:, pl.ds(local_column, tile)],
+                preferred_element_type=f32,
+            )
+
+        part[:, pl.ds(first, tile)] = added[...].astype(part.dtype)
+
+        @pl.when(step + 1 < steps)
+        def _():
+            for load in loads(step + 1, side):
+                load.start()
+
+    def send(step, side):
         if n == 4:
-            for side, slot in ((0, by_y), (1, by_x)):
-                loads.append(
-                    pltpu.make_async_copy(
-                        t_in[i].at[slot, :, cut[side]], t_mid[i].at[side], t_load.at[i, 1 + side]
-                    )
-                )
-        return loads
-
-    def t_direct(i, k, slot, landing):
-        return remote(
-            t_in[i].at[slot],
-            t_got[i].at[landing],
-            t_send.at[i, k],
-            t_recv.at[i, k],
-            {"tensor": lax.rem(me + k, n)},
-        )
-
-    for i in range(nt):
-        if n == 4:
-            for part in range(2):
-                for side in range(2):
-                    t_first(i, side, part).start()
+            t_first(step, side, 0).start()
+            t_first(step, side, 1).start()
         else:
             for k in range(1, n):
-                t_direct(i, k, lax.rem(me + k, n), me).start()
-        for load in t_loads(i):
-            load.start()
+                t_direct(step, side, k, lax.rem(me + k, n), me).start()
 
     for i in range(nd):
         pltpu.make_async_copy(d_in[i].at[:, core], d_own[i], d_load.at[i]).wait()
-        remote(
-            d_in[i].at[:, 1 - core], d_sib[i], s_send.at[i], s_recv.at[i], sibling
-        ).wait_recv()
+        d_pair(i).wait_recv()
         for d in range(pairs):
             d_own[i][d] = (d_own[i][d].astype(f32) + d_sib[i][d].astype(f32)).astype(
                 d_own[i].dtype
@@ -414,19 +452,20 @@
             (right, left)[direction],
         )
 
-    def d_step(j):
+    def d_outer(j):
         for direction, d in ((0, pairs - 1 - j), (1, j)):
-            outer = spot == 0 if direction == 0 else spot == pairs - 1
-            inner = (
-                (spot > 0) & (spot < d) if direction == 0 else (spot < pairs - 1) & (spot > d)
-            )
-
-            @pl.when(outer)
+
+            @pl.when(spot == 0 if direction == 0 else spot == pairs - 1)
             def _(direction=direction, d=d):
                 for i in range(nd):
                     d_copy(i, direction, j, d_own[i].at[d]).start()
 
-            @pl.when(inner)
+    def d_inner(j):
+        for direction, d in ((0, pairs - 1 - j), (1, j)):
+
+            @pl.when(
+                (spot > 0) & (spot < d) if direction == 0 else (spot < pairs - 1) & (spot > d)
+            )
             def _(direction=direction, d=d):
                 for i in range(nd):
                     here = d_side[i].at[direction, j]
@@ -436,40 +475,62 @@
                     )
                     d_copy(i, direction, j, here).start()
 
-    def t_forward(i):
-        loads = t_loads(i)
+    for j in range(pairs - 1):
+        d_outer(j)
+
+    def make(step, carry):
+        compute(step, 0)
+        pl.when(step > 0)(lambda: send(step - 1, 1))
+        compute(step, 1)
+        send(step, 0)
+        return carry
+
+    lax.fori_loop(0, steps, make, 0)
+    send(steps - 1, 1)
+
+    def forward(step, carry):
         for side in range(2):
-            loads[1 + side].wait()
-            t_first(i, side, 0).wait_recv()
-            t_mid[i][side] = (
-                t_mid[i][side].astype(f32) + t_got[i][side, 0].astype(f32)
-            ).astype(t_mid[i].dtype)
-            t_second(i, side).start()
-
-    for j in range(max(pairs - 1, nt)):
-        if j < pairs - 1:
-            d_step(j)
-        if n == 4 and j < nt:
-            t_forward(j)
-
-    for i in range(nt):
-        t_loads(i)[0].wait()
-        if n == 4:
-            for side in range(2):
-                t_first(i, side, 1).wait_recv()
-                t_second(i, side).wait_recv()
-                t_out[i][:, cut[side]] = (
-                    t_own[i][:, cut[side]].astype(f32)
-                    + t_got[i][side, 1].astype(f32)
-                    + t_end[i][side].astype(f32)
-                ).astype(t_out[i].dtype)
-        else:
-            added = t_own[i][...].astype(f32)
-            for k in range(1, n):
-                source = lax.rem(me + n - k, n)
-                t_direct(i, k, me, source).wait_recv()
-                added = added + t_got[i][source].astype(f32)
-            t_out[i][...] = added.astype(t_out[i].dtype)
+            slot = (by_y, by_x)[side]
+            span = pl.ds(pl.multiple_of(step * tile, tile), tile)
+            t_first(step, side, 0).wait_recv()
+            got[side, 0, :, span] = (
+                got[side, 0, :, span].astype(f32)
+                + part[span_of(slot), pl.ds(column(step, side), tile)].astype(f32)
+            ).astype(got.dtype)
+            t_second(step, side).start()
+        return carry
+
+    if pairs > 1:
+        d_inner(0)
+    if n == 4:
+        lax.fori_loop(0, steps, forward, 0)
+    for j in range(1, pairs - 1):
+        d_inner(j)
+
+    def close(step, carry):
+        for side in range(2):
+            here = pl.ds(column(step, side), tile)
+            total_part = part[span_of(me), here].astype(f32)
+            if n == 4:
+                span = pl.ds(pl.multiple_of(step * tile, tile), tile)
+                t_first(step, side, 1).wait_recv()
+                t_second(step, side).wait_recv()
+                total_part = total_part + got[side, 1, :, span].astype(f32)
+                total_part = total_part + end[side, :, span].astype(f32)
+                t_first(step, side, 0).wait_send()
+                t_first(step, side, 1).wait_send()
+                t_second(step, side).wait_send()
+            else:
+                for k in range(1, n):
+                    source = lax.rem(me + n - k, n)
+                    t_direct(step, side, k, me, source).wait_recv()
+                    total_part = total_part + got[source, :, here].astype(f32)
+                for k in range(1, n):
+                    t_direct(step, side, k, lax.rem(me + k, n), me).wait_send()
+            t_out[:, here] = total_part.astype(t_out.dtype)
+        return carry
+
+    lax.fori_loop(0, steps, close, 0)
 
     for i in range(nd):
         d_out[i][...] = d_own[i][spot].astype(f32)
@@ -488,9 +549,7 @@
             d_out[i][...] = d_out[i][...] + here[...].astype(f32)
 
     for i in range(nd):
-        remote(
-            d_in[i].at[:, 1 - core], d_sib[i], s_send.at[i], s_recv.at[i], sibling
-        ).wait_send()
+        d_pair(i).wait_send()
         for j in range(pairs - 1):
             for direction, d in ((0, pairs - 1 - j), (1, j)):
                 pl.when(spot < d if direction == 0 else spot > d)(
@@ -498,53 +557,46 @@
                         i, direction, j, d_side[i].at[direction, j]
                     ).wait_send()
                 )
-    for i in range(nt):
-        if n == 4:
-            for side in range(2):
-                t_first(i, side, 0).wait_send()
-                t_first(i, side, 1).wait_send()
-                t_second(i, side).wait_send()
-        else:
-            for k in range(1, n):
-                t_direct(i, k, lax.rem(me + k, n), me).wait_send()
-
-
-def scatter_all(tensor_arrays, dp_arrays, collective_id):
+
+
+def finish_all(gradient_rows, adapter_rows, down, query_w, key_value_w, dp_arrays, collective_id):
     n, total = lax.axis_size("tensor"), lax.axis_size("dp")
-    nt, nd = len(tensor_arrays), len(dp_arrays)
+    nd = len(dp_arrays)
     pairs = total // 2
-    shaped_t = [a.reshape(n, a.shape[0] // n, a.shape[1]) for a in tensor_arrays]
-    shaped_d = [a.reshape(pairs, 2, a.shape[0] // total, a.shape[1]) for a in dp_arrays]
+    tokens, width = gradient_rows.shape[0], query_w.shape[0]
+    rows, half = tokens // n, width // 2
+    tile = min(512, half, width // n)
+    steps = half // tile
+    shaped = [a.reshape(pairs, 2, a.shape[0] // total, a.shape[1]) for a in dp_arrays]
     dma = pltpu.SemaphoreType.DMA
-    own = [pltpu.VMEM(a.shape[1:], a.dtype) for a in shaped_t]
+    kind = gradient_rows.dtype
     if n == 4:
-        halved = [(a.shape[1], a.shape[2] // 2) for a in shaped_t]
-        kind = [a.dtype for a in shaped_t]
-        mid = [pltpu.VMEM((2,) + h, k) for h, k in zip(halved, kind)]
-        got = [pltpu.VMEM((2, 2) + h, k) for h, k in zip(halved, kind)]
-        end = [pltpu.VMEM((2,) + h, k) for h, k in zip(halved, kind)]
+        landing = [pltpu.VMEM((2, 2, rows, half), kind), pltpu.VMEM((2, rows, half), kind)]
+        flows = 6
     else:
-        mid = [pltpu.VMEM((16, 128), a.dtype) for a in shaped_t]
-        got = [pltpu.VMEM(a.shape, a.dtype) for a in shaped_t]
-        end = [pltpu.VMEM((16, 128), a.dtype) for a in shaped_t]
-    outs = pl.pallas_call(
-        functools.partial(scatter_kernel, n, total, nt, nd),
-        out_shape=[jax.ShapeDtypeStruct(a.shape[1:], a.dtype) for a in shaped_t]
-        + [jax.ShapeDtypeStruct(a.shape[2:], jnp.float32) for a in shaped_d],
-        in_specs=[ANY] * (nt + nd),
-        out_specs=[VMEM] * (nt + nd),
-        scratch_shapes=own
-        + mid
-        + got
-        + end
-        + [pltpu.VMEM((pairs,) + a.shape[2:], a.dtype) for a in shaped_d]
-        + [pltpu.VMEM((pairs,) + a.shape[2:], a.dtype) for a in shaped_d]
-        + [pltpu.VMEM((2, max(pairs - 1, 1)) + a.shape[2:], a.dtype) for a in shaped_d]
+        landing = [pltpu.VMEM((n, rows, width), kind), pltpu.VMEM((16, 128), kind)]
+        flows = 2 * n
+    return pl.pallas_call(
+        functools.partial(finish_kernel, n, total, tile, nd),
+        out_shape=[jax.ShapeDtypeStruct((rows, width), kind)]
+        + [jax.ShapeDtypeStruct(a.shape[2:], jnp.float32) for a in shaped],
+        in_specs=[VMEM] * 3 + [ANY] * (2 + nd),
+        out_specs=[VMEM] * (1 + nd),
+        scratch_shapes=[
+            pltpu.VMEM((tokens, width), kind),
+            pltpu.VMEM((tokens, tile), jnp.float32),
+            *landing,
+            pltpu.VMEM((2, tile, query_w.shape[1]), kind),
+            pltpu.VMEM((2, 2, tile, key_value_w.shape[2]), kind),
+        ]
+        + [pltpu.VMEM((pairs,) + a.shape[2:], a.dtype) for a in shaped]
+        + [pltpu.VMEM((pairs,) + a.shape[2:], a.dtype) for a in shaped]
+        + [pltpu.VMEM((2, max(pairs - 1, 1)) + a.shape[2:], a.dtype) for a in shaped]
         + [
-            dma((nt, 3)),
+            dma((2, 2)),
             dma((nd,)),
-            dma((nt, max(n, 6))),
-            dma((nt, max(n, 6))),
+            dma((flows, steps)),
+            dma((flows, steps)),
             dma((nd, 2, pairs)),
             dma((nd, 2, pairs)),
             dma((nd,)),
@@ -553,9 +605,8 @@
         compiler_params=pltpu.CompilerParams(
             collective_id=collective_id, has_side_effects=True, vmem_limit_bytes=VMEM_BYTES
         ),
-        name="scatter_all",
-    )(*shaped_t, *shaped_d)
-    return outs
+        name="finish_all",
+    )(gradient_rows, adapter_rows, down, query_w, key_value_w, *shaped)
 
 
 adapter_scale = 2.0
@@ -872,24 +923,14 @@
     input_down_gradient = contract_leading_axis(adapter_input_gradient, local_columns).reshape(
         adapter_overall_count, 3 * adapter_rank_rows, narrow_cast
     )
-    adapter_row_values = adapter_input_gradient
-    heads_sum = contract_trailing_axis(query_gradient_rows, query_weight) + contract_trailing_axis(
-        key_gradient_rows, key_value_weight[0]
-    )
-    heads_sum = heads_sum + contract_trailing_axis(value_gradient_rows, key_value_weight[1])
-    adjacent_columns = jnp.dot(
-        adapter_row_values, input_down_flattened, preferred_element_type=jnp.float32
-    )
-    placed = lax.dynamic_update_slice_in_dim(
-        jnp.zeros((lax.axis_size("tensor") * tok_rows, full_width), jnp.float32),
-        adjacent_columns,
-        col_start,
-        1,
-    )
     half = jnp.bfloat16
     wide = lambda grad: grad.reshape(-1, grad.shape[-1]).astype(half)
-    input_grad, *summed = scatter_all(
-        [(heads_sum + placed).astype(half)],
+    input_grad, *summed = finish_all(
+        jnp.concatenate([query_gradient_rows, key_gradient_rows, value_gradient_rows], axis=1),
+        adapter_input_gradient,
+        input_down_flattened,
+        query_weight,
+        key_value_weight,
         [
             wide(input_down_gradient),
             wide(query_up_gradient),

time: 310 us -> 282 us (0.910); the launches traced: 305 us -> 281 us
  matrix products: 127 us -> 85.2 us
  Pallas kernels: 138 us -> 149 us
  local copies, waits for them, and re-layouts: 12.5 us -> 19.4 us
    dot_general x10 -> x7, matrix products: 59 us -> 20.7 us  [contract_trailing_axis(): lax.dot_general(left, right, (((1,), (1,)), ((), ())), preferred_element_...]
    pallas_call x1, Pallas kernels: 70.5 us -> 84.8 us  [finish_all(): pl.pallas_call(functools.partial(finish_kernel, n, total, tile, nd), out_...]
    unnamed x53 -> x85, local copies, waits for them, and re-layouts: 7.84 us -> 7.87 us
  transfers between devices with their start and end apart: 2 -> 2, of which waited for: 1 -> 1; matrix products, arithmetic and copies ran while one was open for 43% -> 35% of each run, Pallas kernels for 28% -> 34%
where the time goes in v2:
time: 282 us; the launch traced here: 281 us
  Pallas kernels  149 us (53%)
  matrix products  85.2 us (30%)
  local copies, waits for them, and re-layouts  19.4 us (7%)
  between operations  14.8 us (5%)
  other arithmetic  11.8 us (4%)
    pallas_call x1, Pallas kernels, finish_all(): pl.pallas_call(functools.partial(finish_kernel, n, total, tile, nd), out_...  84.8 us
    pallas_call x1, Pallas kernels, gather_all(): pl.pallas_call(functools.partial(gather_kernel, n, total, nt, nd), out_sh...  46.9 us
    dot_general x7, matrix products, contract_trailing_axis(): lax.dot_general(left, right, (((1,), (1,)), ((), ())), preferred_element_...  20.7 us
    pallas_call x3, Pallas kernels, small_sum(): pl.pallas_call(functools.partial(small_sum_kernel, n), out_shape=jax.Shap...  17.2 us
    dot_general x1, matrix products, local(): jnp.dot(blended_output, output_weight, preferred_element_type=jnp.float32)  12.8 us
    dot_general x1, matrix products, local(): jnp.dot(gathered, query_weight, preferred_element_type=jnp.float32)  10.1 us
    dot_general x6, matrix products, contract_leading_axis(): lax.dot_general(left, right, (((0,), (0,)), ((), ())), preferred_element_...  8.54 us
    unnamed x85, local copies, waits for them, and re-layouts  7.87 us
  transfers between devices with their start and end apart: 2, of which 1 were waited for; matrix products, arithmetic and copies ran while one was open for 35% of the time, Pallas kernels for 34%

profile of v2, /device:TPU:23, one launch (start us, length us, event | category | flops | bytes accessed | tf_op | source)
XLA Modules:
  0.0 280.7 jit_solution(8631345056992216403)
XLA Ops:
  7.2 46.9 %gather_all.1 = (bf16[4,64,8192]{2,1,0:T(8,128)(2,1)}, bf16[8,2,48,2048]{3,2,1,0:T(8,128)(2,1)}, bf16[8,2,16,1024]{3,2,1,0:T(8,128)(2,1)}, bf16[8,2,2,16,256]{4,...) custom-call(bf16[64,8192]{1,0:T(8,128)(2,1)} %refs_0_.1, ...), custom_call_target="tpu_custom_call" | custom-call | tf_op jit(solution)/shard_map/gather_all/pallas_call | solution.py:240
  54.6 3.9 %fusion.19 = f32[256,48]{0,1:T(8,128)} fusion(bf16[16,48,2048]{2,1,0:T(8,128)(2,1)} %bitcast.228, bf16[256,8192]{1,0:T(8,128)(2,1)} %bitcast.273, s32[]{:T(128)S(6)} %select_n.11, f32[256,16]{0,1:T(8,128)S(1)} %get-tuple-element.63), kind=kOutput, calls=%fused_computation.33 | convolution fusion | flops 805687296 | bytes 4259844 | tf_op jit(solution)/shard_map/dot_general | solution.py:618
  58.5 5.9 %small_sum.3 = f32[48,256]{1,0:T(8,128)} custom-call(f32[48,256]{1,0:T(8,128)} %bitcast.281), custom_call_target="tpu_custom_call" | custom-call | tf_op jit(solution)/shard_map/small_sum/pallas_call | solution.py:295
  64.4 0.8 convert_bitcast_fusion
  65.3 0.3 convolution_multiply_fusion.3
  65.6 10.1 %convolution_add_fusion.1 = f32[256,1024]{1,0:T(8,128)S(1)} fusion(f32[256,1024]{1,0:T(8,128)S(1)} %convolution_multiply_fusion.3, bf16[256,8192]{1,0:T(8,128)(2,1)} %bitcast.274, bf16[8192,1024]{1,0:T(8,128)(2,1)} %refs_3_.3), kind=kOutput, calls=%fused_computation.25 | convolution fusion | flops 4295229440 | bytes 23068672 | tf_op jit(solution)/shard_map/dot_general | solution.py:794
  75.7 0.3 copy.166
  76.1 1.3 reshape_reshape.13
  77.5 0.3 multiply_cosine_fusion
  77.8 0.7 fusion.56
  78.6 5.3 %fusion.7 = f32[256,256]{0,1:T(8,128)S(1)} fusion(bf16[256,8192]{1,0:T(8,128)(2,1)} %bitcast.275, bf16[2,8192,256]{2,1,0:T(8,128)(2,1)} %refs_4_.3), kind=kOutput, calls=%fused_computation.9 | convolution fusion | flops 1073741824 | bytes 8650752 | tf_op jit(solution)/shard_map/dot_general | solution.py:799
  83.9 0.2 fusion.20
  84.2 4.1 %fusion.9 = f32[256,256]{0,1:T(8,128)S(1)} fusion(bf16[256,8192]{1,0:T(8,128)(2,1)S(1)} %bitcast.277, bf16[2,8192,256]{2,1,0:T(8,128)(2,1)} %refs_4_.3), kind=kOutput, calls=%fused_computation.11 | convolution fusion | flops 1073741824 | bytes 8650752 | tf_op jit(solution)/shard_map/dot_general | solution.py:804
  88.3 0.9 fusion.22
  89.2 0.7 fusion.59
  90.0 1.0 fusion.38
  91.0 3.3 %fusion.82 = (f32[2,4,256]{2,1,0:T(4,128)S(1)}, f32[2,4,256,256]{2,3,1,0:T(8,128)}) fusion(pred[256,256]{0,1:T(8,128)(4,1)} %fusion.56, bf16[256,2,128,1]{0,2,3,1:T(8,128)(2,1)} %fusion.59, bf16[256,2,4,128]{0,3,2,1:T(8,128)(2,1)} %fusion.38), kind=kOutput, calls=%fused_computation.143 | convolution fusion | flops 136315136 | bytes 2826240 | tf_op jit(solution)/shard_map/sub | solution.py:682
  94.3 2.0 convolution_convert_fusion.2
  96.3 0.9 fusion.26
  97.2 12.8 %fusion.83 = f32[256,8192]{1,0:T(8,128)} fusion(bf16[256,1024]{0,1:T(8,128)(2,1)S(1)} %bitcast.231, bf16[1024,8192]{1,0:T(8,128)(2,1)} %param.18), kind=kOutput, calls=%fused_computation.144 | convolution fusion | flops 4294967296 | bytes 25690112 | tf_op jit(solution)/shard_map/dot_general | solution.py:854
  110.1 0.4 all-gather.2.cloned.1.call-done
  110.5 3.6 %fusion.33 = f32[256,4]{0,1:T(4,128)S(1)} fusion(bf16[256,8192]{1,0:T(8,128)(2,1)} %all-gather.2.cloned.1.call-done, bf16[16,4,8192]{2,1,0:T(4,128)(2,1)S(1)} %bitcast.255, f32[256,16]{0,1:T(8,128)S(1)} %copy-done.34), kind=kOutput, calls=%fused_computation.55 | convolution fusion | flops 268467200 | bytes 5263360 | tf_op jit(solution)/shard_map/dot_general | solution.py:618
  114.1 0.6 maximum_bitcast_fusion.1.in_ref
  114.8 5.5 %small_sum.4 = f32[32,256]{1,0:T(8,128)} custom-call(f32[32,256]{1,0:T(8,128)} %maximum_bitcast_fusion.1.in_ref), custom_call_target="tpu_custom_call" | custom-call | tf_op jit(solution)/shard_map/small_sum/pallas_call | solution.py:295
  120.3 0.8 convert_bitcast_fusion.1
  121.1 6.6 %fusion.3 = bf16[256,8192]{1,0:T(8,128)(2,1)} fusion(f32[256,8192]{1,0:T(8,128)} %fusion.83, bf16[256,64]{0,1:T(8,128)(2,1)S(1)} %mul.428, bf16[64,8192]{1,0:T(8,128)(2,1)S(1)} %reshape_reshape.13), kind=kOutput, calls=%fused_computation.4 | convolution fusion | flops 274726912 | bytes 13664256 | tf_op jit(solution)/shard_map/dot_general | solution.py:856
  127.8 0.8 copy.132
  128.5 0.8 copy.135
  129.3 0.3 fusion.84
  129.6 0.3 copy-done.9
  130.0 11.6 %fusion.18 = bf16[256,1024]{1,0:T(8,128)(2,1)S(1)} fusion(f32[256,1024]{1,0:T(8,128)S(1)} %fusion.84, bf16[256,8192]{1,0:T(8,128)(2,1)} %all-gather.2.cloned.1.call-done, bf16[1024,8192]{1,0:T(8,128)(2,1)} %param.18), kind=kOutput, calls=%fused_computation.32 | convolution fusion | flops 4295491584 | bytes 22544384 | tf_op jit(solution)/shard_map/dot_general | solution.py:618
  141.7 1.4 fusion.85
  143.2 3.2 %convolution_bitcast_fusion.1 = f32[256,2,128]{0,2,1:T(8,128)S(1)} fusion(bf16[256,2,4,128]{0,3,2,1:T(8,128)(2,1)} %fusion.38, f32[2,256,256,4]{2,1,3,0:T(8,128)S(1)} %fusion.85, f32[2,4,256,256]{2,3,1,0:T(8,128)} %get-tuple-element.65, f32[2,4,256]{2,1,0:T(4,128)S(1)} %get-tuple-element.64), kind=kOutput, calls=%fused_computation.45 | convolution fusion | flops 137890048 | bytes 4988928 | tf_op jit(solution)/shard_map/gpts,tgpe->sge/dot_general | solution.py:712
  146.5 0.8 copy.171
  147.6 2.1 fusion.25
  149.7 0.8 copy.172
  150.8 0.7 copy.147
  151.6 3.3 %fusion.46 = f32[2,128,4,256]{3,1,2,0:T(8,128)S(1)} fusion(bf16[256,2,128,1]{0,2,3,1:T(8,128)(2,1)} %fusion.59, f32[2,256,256,4]{2,1,3,0:T(8,128)S(1)} %fusion.85, f32[2,4,256,256]{2,3,1,0:T(8,128)} %get-tuple-element.65, f32[2,4,256]{2,1,0:T(4,128)S(1)} %get-tuple-element.64), kind=kOutput, calls=%fused_computation.72 | convolution fusion | flops 137890048 | bytes 5382144 | tf_op jit(solution)/shard_map/gpts,sge->tgpe/dot_general | solution.py:709
  154.8 0.9 fusion.78
  155.7 0.4 copy.176
  156.2 1.5 copy.177
  157.7 1.7 broadcast_multiply_fusion
  159.4 1.6 copy.141
  161.5 0.4 fusion.40
  161.9 0.4 copy-done.20
  162.3 0.3 fusion.27
  162.6 0.6 maximum_bitcast_fusion.in_ref
  163.3 5.9 %small_sum.5 = f32[48,256]{1,0:T(8,128)} custom-call(f32[48,256]{1,0:T(8,128)} %maximum_bitcast_fusion.in_ref), custom_call_target="tpu_custom_call" | custom-call | tf_op jit(solution)/shard_map/small_sum/pallas_call | solution.py:295
  169.1 0.8 fusion.62
  170.0 0.9 copy.148.refs_1_
  170.9 0.3 copy.170
  171.4 1.7 fusion.36
  173.0 0.9 pad_maximum_fusion.1.refs_0_
  174.0 1.1 convolution_convert_fusion.1
  175.1 1.1 fusion.17
  176.3 4.0 %convolution_convert_fusion = bf16[768,2048]{1,0:T(8,128)(2,1)} fusion(bf16[256,768]{0,1:T(8,128)(2,1)S(1)} %bitcast.223, bf16[256,8192]{1,0:T(8,128)(2,1)} %bitcast.276, s32[]{:T(128)S(6)} %select_n.11), kind=kOutput, calls=%fused_computation.15 | convolution fusion | flops 806879232 | bytes 4587524 | tf_op jit(solution)/shard_map/dot_general | solution.py:624
  180.3 1.8 fusion.4
  182.1 84.8 %finish_all.1 = (bf16[64,8192]{1,0:T(8,128)(2,1)}, f32[96,2048]{1,0:T(8,128)}, f32[32,1024]{1,0:T(8,128)}, f32[64,256]{1,0:T(8,128)}, f32[32,1024]{1,0:T(8,128)}, /*index=5*/f32[8,8192]{1,0:T(8,128)}) custom-call(bf16[256,1536]{1,0:T(8,128)(2,1)} %pad_maximum_fusion.1.refs_0_, bf16[256,768]{1,0:T(8,128)(2,1)} %copy.148.refs_1_, bf16[768,2048]{1,0:T(8,128)(2,1)} %bitcast.229, ...), custom_call_target="tpu_custom_call" | custom-call | tf_op jit(solution)/shard_map/finish_all/pallas_call | solution.py:579
  266.9 1.8 reshape.367
  268.7 2.3 copy.191
  271.0 0.9 copy.192
  271.9 0.7 copy.193
  272.6 0.6 copy.194
  273.2 0.7 copy.195
  (113 shorter events, 2.4 us)
Async XLA Ops:
  7.2 47.1 %copy-start.38 = (s32[1,8]{1,0:T(1,128)S(1)}, s32[1,8]{1,0:T(1,128)}, u32[]{:S(2)}) copy-start(s32[1,8]{1,0:T(1,128)} %param.14) | copy-start | bytes 100
  7.2 47.3 %copy-start.37 = (s32[1,8]{1,0:T(1,128)S(1)}, s32[1,8]{1,0:T(1,128)}, u32[]{:S(2)}) copy-start(s32[1,8]{1,0:T(1,128)} %param.15) | copy-start | bytes 100
  7.2 103.3 %all-gather.2.cloned.1.call-start = ((), (), s32[]{:S(2)}) async-start(), calls=%async_computation.1 | async-start | bytes 5242880 | tf_op jit(solution)/shard_map/all_gather | solution.py:755
  54.2 214.5 %reduce-scatter.2.cloned.1.call-start = ((), (), s32[]{:S(2)}) async-start(), calls=%async_computation.2 | async-start | bytes 5242880 | tf_op jit(solution)/shard_map/reduce_scatter | solution.py:852
  54.6 3.9 %copy-start.32 = (f32[256,16]{0,1:T(8,128)}, f32[256,16]{0,1:T(8,128)S(1)}, u32[]{:S(2)}) copy-start(f32[256,16]{0,1:T(8,128)S(1)} %get-tuple-element.63) | copy-start | bytes 49156
  54.6 10.7 %copy-start.19 = (bf16[8,2,16,1024]{3,2,1,0:T(8,128)(2,1)S(1)}, bf16[8,2,16,1024]{3,2,1,0:T(8,128)(2,1)}, u32[]{:S(2)}) copy-start(bf16[8,2,16,1024]{3,2,1,0:T(8,128)(2,1)} %get-tuple-element.25) | copy-start | bytes 1572868
  65.2 10.5 %copy-start.7 = (bf16[256,16,16]{0,2,1:T(8,128)(2,1)}, bf16[256,16,16]{0,2,1:T(8,128)(2,1)S(1)}, u32[]{:S(2)}) copy-start(bf16[256,16,16]{0,2,1:T(8,128)(2,1)S(1)} %get-tuple-element.57) | copy-start | bytes 393220
  65.2 18.7 %copy-start.5 = (bf16[256,16,16]{0,2,1:T(8,128)(2,1)}, bf16[256,16,16]{0,2,1:T(8,128)(2,1)S(1)}, u32[]{:S(2)}) copy-start(bf16[256,16,16]{0,2,1:T(8,128)(2,1)S(1)} %get-tuple-element.58) | copy-start | bytes 393220
  75.7 2.8 %copy-start.26 = (bf16[8,2,2,16,256]{4,3,2,1,0:T(8,128)(2,1)S(1)}, bf16[8,2,2,16,256]{4,3,2,1,0:T(8,128)(2,1)}, u32[]{:S(2)}) copy-start(bf16[8,2,2,16,256]{4,3,2,1,0:T(8,128)(2,1)} %get-tuple-element.24) | copy-start | bytes 786436
  78.6 5.6 %copy-start.28 = (bf16[4,64,8192]{2,1,0:T(8,128)(2,1)S(1)}, bf16[4,64,8192]{2,1,0:T(8,128)(2,1)}, u32[]{:S(2)}) copy-start(bf16[4,64,8192]{2,1,0:T(8,128)(2,1)} %get-tuple-element.21) | copy-start | bytes 12582916
  91.0 3.3 %copy-start.23 = (bf16[256,256]{0,1:T(8,128)(2,1)S(1)}, bf16[256,256]{0,1:T(8,128)(2,1)}, u32[]{:S(2)}) copy-start(bf16[256,256]{0,1:T(8,128)(2,1)} %fusion.22) | copy-start | bytes 393220
  94.3 2.0 copy-start.21
  94.3 2.0 copy-start.33
  96.3 13.8 %copy-start.1 = (bf16[2,128,4,256]{3,1,2,0:T(8,128)(2,1)}, bf16[2,128,4,256]{3,1,2,0:T(8,128)(2,1)S(1)}, u32[]{:S(2)}) copy-start(bf16[2,128,4,256]{3,1,2,0:T(8,128)(2,1)S(1)} %convolution_convert_fusion.2) | copy-start | bytes 1572868
  97.2 13.2 %copy-start.11 = (bf16[8,2,4,8192]{3,2,1,0:T(4,128)(2,1)S(1)}, bf16[8,2,4,8192]{3,2,1,0:T(4,128)(2,1)}, u32[]{:S(2)}) copy-start(bf16[8,2,4,8192]{3,2,1,0:T(4,128)(2,1)} %get-tuple-element.28) | copy-start | bytes 3145732
  97.2 13.2 %copy-start.34 = (f32[256,16]{0,1:T(8,128)S(1)}, f32[256,16]{0,1:T(8,128)}, u32[]{:S(2)}) copy-start(f32[256,16]{0,1:T(8,128)} %copy-done.32) | copy-start | bytes 49156
  110.5 3.7 %copy-start.36 = (f32[256,16]{0,1:T(8,128)S(1)}, f32[256,16]{0,1:T(8,128)}, u32[]{:S(2)}) copy-start(f32[256,16]{0,1:T(8,128)} %fusion.26) | copy-start | bytes 49156
  121.1 6.7 %copy-start.24 = (bf16[256,64]{0,1:T(8,128)(2,1)}, bf16[256,64]{0,1:T(8,128)(2,1)S(1)}, u32[]{:S(2)}) copy-start(bf16[256,64]{0,1:T(8,128)(2,1)S(1)} %mul.428) | copy-start | bytes 98308
  127.7 1.6 copy-start.22
  129.3 0.7 copy-start.9
  143.2 4.1 %copy-start.6 = (bf16[256,16,16]{0,2,1:T(8,128)(2,1)S(1)}, bf16[256,16,16]{0,2,1:T(8,128)(2,1)}, u32[]{:S(2)}) copy-start(bf16[256,16,16]{0,2,1:T(8,128)(2,1)} %copy-done.5) | copy-start | bytes 393220
  146.5 3.2 %copy-start.3 = (bf16[256,2,128]{0,2,1:T(8,128)(2,1)}, bf16[256,2,128]{0,2,1:T(8,128)(2,1)S(1)}, u32[]{:S(2)}) copy-start(bf16[256,2,128]{0,2,1:T(8,128)(2,1)S(1)} %fusion.55) | copy-start | bytes 393220
  149.7 1.1 copy-start.17
  156.1 1.6 copy-start.16
  159.4 1.7 copy-start.4
  159.4 1.7 copy-start.27
  159.4 1.7 copy-start.35
  159.4 1.9 copy-start.18
  161.3 1.0 copy-start.20
  162.6 8.6 %copy-start.13 = (f32[256,128]{1,0:T(8,128)S(1)}, f32[256,128]{1,0:T(8,128)}, u32[]{:S(2)}) copy-start(f32[256,128]{1,0:T(8,128)} %copy.132) | copy-start | bytes 393220
  171.3 1.7 copy-start.14
  171.3 1.7 copy-start.15
  171.3 2.6 copy-start.2
  171.4 2.6 copy-start.10
  173.0 2.1 copy-start.8
  176.3 4.0 %copy-start = (bf16[256,8192]{1,0:T(8,128)(2,1)S(1)}, bf16[256,8192]{1,0:T(8,128)(2,1)}, u32[]{:S(2)}) copy-start(bf16[256,8192]{1,0:T(8,128)(2,1)} %all-gather.2.cloned.1.call-done) | copy-start | bytes 12582916
  176.3 4.0 %copy-start.25 = (bf16[256,64]{0,1:T(8,128)(2,1)S(1)}, bf16[256,64]{0,1:T(8,128)(2,1)}, u32[]{:S(2)}) copy-start(bf16[256,64]{0,1:T(8,128)(2,1)} %copy-done.24) | copy-start | bytes 98308
  266.9 4.1 %copy-start.12 = (f32[96,2048]{1,0:T(8,128)S(1)}, f32[96,2048]{1,0:T(8,128)}, u32[]{:S(2)}) copy-start(f32[96,2048]{1,0:T(8,128)} %get-tuple-element.30) | copy-start | bytes 2359300
  266.9 5.0 %copy-start.30 = (f32[32,1024]{1,0:T(8,128)S(1)}, f32[32,1024]{1,0:T(8,128)}, u32[]{:S(2)}) copy-start(f32[32,1024]{1,0:T(8,128)} %get-tuple-element.31) | copy-start | bytes 393220
  268.7 3.9 %copy-start.31 = (f32[64,256]{1,0:T(8,128)S(1)}, f32[64,256]{1,0:T(8,128)}, u32[]{:S(2)}) copy-start(f32[64,256]{1,0:T(8,128)} %get-tuple-element.32) | copy-start | bytes 196612
  268.7 4.5 %copy-start.29 = (f32[32,1024]{1,0:T(8,128)S(1)}, f32[32,1024]{1,0:T(8,128)}, u32[]{:S(2)}) copy-start(f32[32,1024]{1,0:T(8,128)} %get-tuple-element.33) | copy-start | bytes 393220
Sparse Core Ops, SparseCore 0:
  54.3 56.1 all-gather.1
  127.9 58.4 reduce-scatter.1

commit v3 on v2

--- a/solution.py
+++ b/solution.py
@@ -63,8 +63,10 @@
     take = iter(refs)
     t_in = [next(take) for _ in range(nt)]
     d_in = [next(take) for _ in range(nd)]
+    query_w, key_value_w = next(take), next(take)
     t_out = [next(take) for _ in range(nt)]
     d_out = [next(take) for _ in range(nd)]
+    projected, held, query_buf, key_value_buf, w_sem, h_sem = (next(take) for _ in range(6))
     stage = [next(take) for _ in range(nt + nd)]
     load_sem, store_sem, t_send, t_recv, d_send, d_recv, s_send, s_recv = take
     pairs = total // 2
@@ -74,6 +76,49 @@
     right, left = {"dp": (spot + 1) * 2 + core}, {"dp": (spot - 1) * 2 + core}
     peers = tensor_peers(n)
     me = peers[0]
+
+    rows = t_in[0].shape[0]
+    depth = query_buf.shape[1]
+    steps = t_in[0].shape[1] // depth
+    query_columns = query_w.shape[1]
+    key_value_columns = key_value_w.shape[2]
+
+    def loads(step):
+        span, slot = pl.ds(pl.multiple_of(step * depth, depth), depth), lax.rem(step, 2)
+        return (
+            pltpu.make_async_copy(query_w.at[span, :], query_buf.at[slot], w_sem.at[slot, 0]),
+            pltpu.make_async_copy(
+                key_value_w.at[:, span, :], key_value_buf.at[slot], w_sem.at[slot, 1]
+            ),
+        )
+
+    def hold(k):
+        slot = lax.rem(me + k, n)
+        source = t_in[0] if k == 0 else t_out[0].at[slot]
+        target = held.at[pl.ds(pl.multiple_of(slot * rows, rows), rows)]
+        return pltpu.make_async_copy(source, target, h_sem.at[k])
+
+    def project(step, carry):
+        for load in loads(step):
+            load.wait()
+
+        @pl.when(step + 1 < steps)
+        def _():
+            for load in loads(step + 1):
+                load.start()
+
+        slot = lax.rem(step, 2)
+        chunk = held[:, pl.ds(pl.multiple_of(step * depth, depth), depth)]
+        at = query_columns
+        for weights, first, width in (
+            (query_buf[slot], 0, query_columns),
+            (key_value_buf[slot, 0], at, key_value_columns),
+            (key_value_buf[slot, 1], at + key_value_columns, key_value_columns),
+        ):
+            projected[:, first : first + width] += jnp.dot(
+                chunk, weights, preferred_element_type=jnp.float32
+            )
+        return carry
 
     greet(tensor_devices(n) + dp_devices(total))
 
@@ -191,17 +236,31 @@
             t_copy(i, 4).start()
             t_arrival(i, 1).wait_recv()
             t_copy(i, 5).start()
-    for step in range(1, pairs):
+    hold(0).start()
+    for load in loads(0):
+        load.start()
+    projected[...] = jnp.zeros_like(projected)
+    for step in range(1, max(pairs - 1, 1)):
         dp_step(step)
     for i in range(nt):
         if n == 4:
             for which in range(2, 6):
                 t_arrival(i, which).wait_recv()
+        else:
+            for k in range(1, n):
+                t_direct(i, k, lax.rem(me + n - k, n)).wait_recv()
+    for k in range(1, n):
+        hold(k).start()
+    for k in range(n):
+        hold(k).wait()
+    lax.fori_loop(0, steps, project, 0)
+    if pairs > 1:
+        dp_step(pairs - 1)
+    for i in range(nt):
+        if n == 4:
             for which in range(6):
                 t_copy(i, which).wait_send()
         else:
-            for k in range(1, n):
-                t_direct(i, k, lax.rem(me + n - k, n)).wait_recv()
             for k in range(1, n):
                 t_direct(i, k, me).wait_send()
     for i in range(nd):
@@ -230,21 +289,32 @@
         pltpu.make_async_copy(stage[i], target, store_sem.at[i]).wait()
 
 
-def gather_all(tensor_arrays, dp_arrays, collective_id):
+def gather_all(tensor_arrays, dp_arrays, query_w, key_value_w, collective_id):
     n, total = lax.axis_size("tensor"), lax.axis_size("dp")
     nt, nd = len(tensor_arrays), len(dp_arrays)
     pairs = total // 2
     every = list(tensor_arrays) + list(dp_arrays)
     lead = [n] * nt + [total] * nd
     dma = pltpu.SemaphoreType.DMA
+    tokens, width = tensor_arrays[0].shape[0] * n, tensor_arrays[0].shape[1]
+    columns = query_w.shape[1] + 2 * key_value_w.shape[2]
+    depth = min(1024, width)
     outs = pl.pallas_call(
         functools.partial(gather_kernel, n, total, nt, nd),
         out_shape=[
             jax.ShapeDtypeStruct((count,) + a.shape, a.dtype) for count, a in zip(lead, every)
-        ],
-        in_specs=[ANY] * (nt + nd),
-        out_specs=[ANY] * (nt + nd),
-        scratch_shapes=[pltpu.VMEM(a.shape, a.dtype) for a in every]
+        ]
+        + [jax.ShapeDtypeStruct((tokens, columns), jnp.float32)],
+        in_specs=[ANY] * (nt + nd + 2),
+        out_specs=[ANY] * (nt + nd) + [VMEM],
+        scratch_shapes=[
+            pltpu.VMEM((tokens, width), query_w.dtype),
+            pltpu.VMEM((2, depth, query_w.shape[1]), query_w.dtype),
+            pltpu.VMEM((2, 2, depth, key_value_w.shape[2]), query_w.dtype),
+            dma((2, 2)),
+            dma((n,)),
+        ]
+        + [pltpu.VMEM(a.shape, a.dtype) for a in every]
         + [
             dma((nt + nd,)),
             dma((nt + nd,)),
@@ -259,8 +329,9 @@
             collective_id=collective_id, has_side_effects=True, vmem_limit_bytes=VMEM_BYTES
         ),
         name="gather_all",
-    )(*every)
-    return [o.reshape((o.shape[0] * o.shape[1],) + o.shape[2:]) for o in outs]
+    )(*every, query_w, key_value_w)
+    *outs, projected = outs
+    return [projected] + [o.reshape((o.shape[0] * o.shape[1],) + o.shape[2:]) for o in outs]
 
 
 def small_sum_kernel(n, in_ref, out_ref, slots, send_sem, recv_sem):
@@ -740,6 +811,7 @@
     query_columns = query_weight.shape[1]
     key_value_columns = key_value_weight.shape[2]
     (
+        projected,
         gathered,
         input_down_every,
         query_up_every,
@@ -749,6 +821,8 @@
     ) = gather_all(
         [hidden_in],
         [a_in, b_query, b_key_value, output_down_factor, output_up_factor],
+        query_weight,
+        key_value_weight,
         0,
     )
     out_grad, gathered = lax.optimization_barrier((out_grad, gathered))
@@ -791,19 +865,15 @@
     adapter_value_delta = expand_from_rank(
         onehot_halfprec, input_rank_rows[:, 2 * adapter_rank_rows :]
     )
-    query_before_rotation = jnp.dot(
-        gathered, query_weight, preferred_element_type=jnp.float32
-    ) + adapter_scale * jnp.dot(
+    query_before_rotation = projected[:, :query_columns] + adapter_scale * jnp.dot(
         adapter_query_delta, query_up_flattened, preferred_element_type=jnp.float32
     )
-    key_before_rotation = jnp.dot(
-        gathered, key_value_weight[0], preferred_element_type=jnp.float32
-    ) + adapter_scale * jnp.dot(
+    key_before_rotation = projected[
+        :, query_columns : query_columns + key_value_columns
+    ] + adapter_scale * jnp.dot(
         adapter_key_delta, key_up_flattened, preferred_element_type=jnp.float32
     )
-    value_projected = jnp.dot(
-        gathered, key_value_weight[1], preferred_element_type=jnp.float32
-    ) + adapter_scale * jnp.dot(
+    value_projected = projected[:, query_columns + key_value_columns :] + adapter_scale * jnp.dot(
         adapter_value_delta, value_up_flattened, preferred_element_type=jnp.float32
     )
     queries = apply_rotation(
@@ -872,6 +942,20 @@
     output_down_gradient = contract_leading_axis(adapter_output_gradient, blended_output).reshape(
         adapter_overall_count, adapter_rank_rows, query_columns
     )
+    half = jnp.bfloat16
+    wide = lambda grad: grad.reshape(-1, grad.shape[-1]).astype(half)
+    early = jnp.concatenate(
+        [
+            output_down_gradient.astype(half),
+            output_up_gradient.astype(half).reshape(adapter_overall_count, -1, query_columns),
+        ],
+        axis=1,
+    )
+    summed_early = lax.psum_scatter(early, "dp", scatter_dimension=0, tiled=True).astype(
+        jnp.float32
+    )
+    summed_a_out = summed_early[:, :adapter_rank_rows]
+    summed_b_out = summed_early[:, adapter_rank_rows:].reshape(output_up_factor.shape)
     grad_queries, grad_keys, grad_values = attend_back(
         queries, rotated_keys, incoming_values, probs, probs_bf, blended_gradient
     )
@@ -923,8 +1007,6 @@
     input_down_gradient = contract_leading_axis(adapter_input_gradient, local_columns).reshape(
         adapter_overall_count, 3 * adapter_rank_rows, narrow_cast
     )
-    half = jnp.bfloat16
-    wide = lambda grad: grad.reshape(-1, grad.shape[-1]).astype(half)
     input_grad, *summed = finish_all(
         jnp.concatenate([query_gradient_rows, key_gradient_rows, value_gradient_rows], axis=1),
         adapter_input_gradient,
@@ -935,16 +1017,12 @@
             wide(input_down_gradient),
             wide(query_up_gradient),
             wide(grad_b_kv),
-            wide(output_down_gradient),
-            wide(output_up_gradient),
         ],
         4,
     )
-    summed_a_in, summed_b_query, summed_b_kv, summed_a_out, summed_b_out = [
+    summed_a_in, summed_b_query, summed_b_kv = [
         s.reshape(factor.shape)
-        for s, factor in zip(
-            summed, (a_in, b_query, b_key_value, output_down_factor, output_up_factor)
-        )
+        for s, factor in zip(summed, (a_in, b_query, b_key_value))
     ]
     return (
         attn_out,

time: 282 us -> 291 us (1.032)
  waiting for transfers between devices: 0.46 us -> 26.8 us
  matrix products: 85.2 us -> 60.9 us
  local copies, waits for them, and re-layouts: 19.4 us -> 27.6 us
  Pallas kernels: 149 us -> 142 us
  other arithmetic: 11.8 us -> 16 us
    all_gather x1, waiting for transfers between devices: 0.43 us -> 26.7 us  [local(): incoming_gradient = lax.all_gather(out_grad, 'tensor', axis=0, tiled=True)]
    dot_general x3 -> x0, matrix products: 19.5 us -> none  [the longest x1 10.1 us: local(): jnp.dot(gathered, query_weight, preferred_element_type=jnp.float32)]
    pallas_call x1, Pallas kernels: 84.8 us -> 66.6 us  [finish_all(): pl.pallas_call(functools.partial(finish_kernel, n, total, tile, nd), out_...]
    pallas_call x1, Pallas kernels: 46.9 us -> 54.7 us  [gather_all(): pl.pallas_call(functools.partial(gather_kernel, n, total, nt, nd), out_sh...]
    unnamed x85 -> x78, local copies, waits for them, and re-layouts: 7.87 us -> 13.9 us
    dot_general x1, matrix products: 12.8 us -> 8.37 us  [local(): jnp.dot(blended_output, output_weight, preferred_element_type=jnp.float32)]
    dot_general x1, matrix products: 6.64 us -> 3.24 us  [local(): jnp.dot(adapter_row_values, output_up_flattened, preferred_element_type=j...]
    pallas_call x3, Pallas kernels: 17.2 us -> 20.2 us  [small_sum(): pl.pallas_call(functools.partial(small_sum_kernel, n), out_shape=jax.Shap...]
  transfers between devices with their start and end apart: 2 -> 3, of which waited for: 1 -> 1; matrix products, arithmetic and copies ran while one was open for 35% -> 30% of each run, Pallas kernels for 34% -> 28%
where the time goes in v3:
time: 291 us; the launch traced here: 287 us
  Pallas kernels  142 us (49%)
  matrix products  60.9 us (21%)
  local copies, waits for them, and re-layouts  27.6 us (9%)
  waiting for transfers between devices  26.8 us (9%)
  other arithmetic  16 us (5%)
  between operations  14.4 us (5%)
    pallas_call x1, Pallas kernels, finish_all(): pl.pallas_call(functools.partial(finish_kernel, n, total, tile, nd), out_...  66.6 us
    pallas_call x1, Pallas kernels, gather_all(): pl.pallas_call(functools.partial(gather_kernel, n, total, nt, nd), out_sh...  54.7 us
    all_gather x1, waiting for transfers between devices, local(): incoming_gradient = lax.all_gather(out_grad, 'tensor', axis=0, tiled=True)  26.7 us
    dot_general x7, matrix products, contract_trailing_axis(): lax.dot_general(left, right, (((1,), (1,)), ((), ())), preferred_element_...  22.3 us
    pallas_call x3, Pallas kernels, small_sum(): pl.pallas_call(functools.partial(small_sum_kernel, n), out_shape=jax.Shap...  20.2 us
    unnamed x78, local copies, waits for them, and re-layouts  13.9 us
    dot_general x6, matrix products, contract_leading_axis(): lax.dot_general(left, right, (((0,), (0,)), ((), ())), preferred_element_...  8.87 us
    dot_general x1, matrix products, local(): jnp.dot(blended_output, output_weight, preferred_element_type=jnp.float32)  8.37 us
  transfers between devices with their start and end apart: 3, of which 1 were waited for; matrix products, arithmetic and copies ran while one was open for 30% of the time, Pallas kernels for 28%

profile of v3, /device:TPU:23, one launch (start us, length us, event | category | flops | bytes accessed | tf_op | source)
XLA Modules:
  0.0 287.4 jit_solution(12472073034700298932)
XLA Ops:
  7.2 54.7 %gather_all.1 = (bf16[4,64,8192]{2,1,0:T(8,128)(2,1)}, bf16[8,2,48,2048]{3,2,1,0:T(8,128)(2,1)}, bf16[8,2,16,1024]{3,2,1,0:T(8,128)(2,1)}, bf16[8,2,2,16,256]{4,...) custom-call(bf16[64,8192]{1,0:T(8,128)(2,1)} %refs_0_.1, ...), custom_call_target="tpu_custom_call" | custom-call | tf_op jit(solution)/shard_map/gather_all/pallas_call | solution.py:302
  62.3 3.9 %fusion.14 = f32[256,48]{0,1:T(8,128)} fusion(bf16[16,48,2048]{2,1,0:T(8,128)(2,1)} %bitcast.218, bf16[256,8192]{1,0:T(8,128)(2,1)} %bitcast.261, s32[]{:T(128)S(6)} %select_n.11, f32[256,16]{0,1:T(8,128)S(1)} %get-tuple-element.61), kind=kOutput, calls=%fused_computation.28 | convolution fusion | flops 805687296 | bytes 4259844 | tf_op jit(solution)/shard_map/dot_general | solution.py:689
  66.2 6.0 %small_sum.3 = f32[48,256]{1,0:T(8,128)} custom-call(f32[48,256]{1,0:T(8,128)} %bitcast.265), custom_call_target="tpu_custom_call" | custom-call | tf_op jit(solution)/shard_map/small_sum/pallas_call | solution.py:366
  72.2 0.8 convert_bitcast_fusion
  73.1 0.6 copy-done.6
  73.7 1.2 fusion.17
  74.9 0.7 convert_element_type.141
  75.6 1.2 fusion.15
  77.0 1.5 fusion.11
  79.1 0.3 fusion.78
  79.5 1.2 copy.194
  80.6 1.9 neg.29
  82.5 0.4 copy.136
  83.3 0.7 fusion.51
  84.1 0.7 fusion.54
  85.0 0.7 copy-done.27
  85.7 3.1 %fusion.82 = (f32[2,4,256]{2,1,0:T(4,128)S(1)}, f32[2,4,256,256]{2,3,1,0:T(8,128)}) fusion(pred[256,256]{0,1:T(8,128)(4,1)} %fusion.51, bf16[256,2,128,1]{0,2,3,1:T(8,128)(2,1)S(1)} %copy-done.27, bf16[256,2,4,128]{0,3,2,1:T(8,128)(2,1)S(1)} %fusion.33), kind=kOutput, calls=%fused_computation.142 | convolution fusion | flops 136315136 | bytes 2826240 | tf_op jit(solution)/shard_map/sub | solution.py:753
  88.8 2.0 convolution_convert_fusion.2
  91.1 26.7 %all-gather.2.cloned.1.call-done = bf16[256,8192]{1,0:T(8,128)(2,1)} async-done(((bf16[64,8192]{1,0:T(8,128)(2,1)}), bf16[256,8192]{1,0:T(8,128)(2,1)}) %all-gather.2.cloned.1.call-update) | async-done | bytes 4194320 | tf_op jit(solution)/shard_map/all_gather | solution.py:829
  117.8 3.6 %fusion.28 = f32[256,4]{0,1:T(4,128)S(1)} fusion(bf16[256,8192]{1,0:T(8,128)(2,1)} %all-gather.2.cloned.1.call-done, bf16[16,4,8192]{2,1,0:T(4,128)(2,1)S(1)} %bitcast.242, f32[256,16]{0,1:T(8,128)S(1)} %copy-done.31), kind=kOutput, calls=%fused_computation.50 | convolution fusion | flops 268467200 | bytes 5263360 | tf_op jit(solution)/shard_map/dot_general | solution.py:689
  121.5 0.6 maximum_bitcast_fusion.1.in_ref
  122.1 5.5 %small_sum.4 = f32[32,256]{1,0:T(8,128)} custom-call(f32[32,256]{1,0:T(8,128)} %maximum_bitcast_fusion.1.in_ref), custom_call_target="tpu_custom_call" | custom-call | tf_op jit(solution)/shard_map/small_sum/pallas_call | solution.py:366
  127.6 0.8 convert_bitcast_fusion.1
  128.4 3.0 %fusion.4 = bf16[64,8192]{1,0:T(8,128)(2,1)S(1)} fusion(bf16[256,64]{0,1:T(8,128)(2,1)S(1)} %mul.425, bf16[256,8192]{1,0:T(8,128)(2,1)} %all-gather.2.cloned.1.call-done), kind=kOutput, calls=%fused_computation.6 | convolution fusion | flops 269484032 | bytes 5275648 | tf_op jit(solution)/shard_map/dot_general | solution.py:695
  131.4 0.5 convert_element_type.171
  132.3 1.4 pad_maximum_fusion
  133.8 1.1 copy-done.13
  135.2 8.4 %fusion.83 = f32[256,8192]{1,0:T(8,128)S(1)} fusion(bf16[256,1024]{0,1:T(8,128)(2,1)S(1)} %bitcast.222, bf16[1024,8192]{1,0:T(8,128)(2,1)} %param.18), kind=kOutput, calls=%fused_computation.143 | convolution fusion | flops 4294967296 | bytes 25690112 | tf_op jit(solution)/shard_map/dot_general | solution.py:924
  143.6 3.2 %fusion.3 = bf16[256,8192]{1,0:T(8,128)(2,1)} fusion(f32[256,8192]{1,0:T(8,128)S(1)} %fusion.83, bf16[256,64]{0,1:T(8,128)(2,1)S(1)} %mul.425, bf16[64,8192]{1,0:T(8,128)(2,1)S(1)} %reshape_reshape.13), kind=kOutput, calls=%fused_computation.4 | convolution fusion | flops 274726912 | bytes 13664256 | tf_op jit(solution)/shard_map/dot_general | solution.py:926
  146.8 0.8 copy.147
  148.2 11.7 %fusion.13 = bf16[256,1024]{1,0:T(8,128)(2,1)S(1)} fusion(f32[256,1024]{1,0:T(8,128)S(1)} %fusion.84, bf16[256,8192]{1,0:T(8,128)(2,1)} %all-gather.2.cloned.1.call-done, bf16[1024,8192]{1,0:T(8,128)(2,1)} %param.18), kind=kOutput, calls=%fused_computation.27 | convolution fusion | flops 4295491584 | bytes 22544384 | tf_op jit(solution)/shard_map/dot_general | solution.py:689
  160.2 2.1 fusion.20
  162.3 0.6 copy-done.18
  162.9 0.8 copy.188
  163.7 0.4 fusion.59
  164.1 3.2 %convolution_bitcast_fusion.1 = f32[256,2,128]{0,2,1:T(8,128)S(1)} fusion(bf16[256,2,4,128]{0,3,2,1:T(8,128)(2,1)} %copy-done.24, f32[2,256,256,4]{2,1,3,0:T(8,128)S(1)} %fusion.59, f32[2,4,256,256]{2,3,1,0:T(8,128)} %get-tuple-element.63, f32[2,4,256]{2,1,0:T(4,128)S(1)} %get-tuple-element.62), kind=kOutput, calls=%fused_computation.40 | convolution fusion | flops 137890048 | bytes 4988928 | tf_op jit(solution)/shard_map/gpts,tgpe->sge/dot_general | solution.py:783
  167.4 0.8 copy.187
  168.1 3.1 %fusion.41 = f32[2,128,4,256]{3,1,2,0:T(8,128)S(1)} fusion(bf16[256,2,128,1]{0,2,3,1:T(8,128)(2,1)} %fusion.54, f32[2,256,256,4]{2,1,3,0:T(8,128)S(1)} %fusion.59, f32[2,4,256,256]{2,3,1,0:T(8,128)} %get-tuple-element.63, f32[2,4,256]{2,1,0:T(4,128)S(1)} %get-tuple-element.62), kind=kOutput, calls=%fused_computation.67 | convolution fusion | flops 137890048 | bytes 5382144 | tf_op jit(solution)/shard_map/gpts,sge->tgpe/dot_general | solution.py:780
  171.5 1.1 fusion.77
  172.6 1.5 copy.195
  174.1 1.0 neg.30
  175.1 2.4 copy.196
  177.5 2.9 %broadcast_multiply_fusion = (f32[256,8,128]{2,1,0:T(8,128)S(1)}, f32[256,8,128]{2,1,0:T(8,128)}) fusion(f32[256,128]{1,0:T(8,128)S(1)} %copy.150, f32[256,8,64]{2,1,0:T(8,128)} %copy.196, f32[256,8,64]{2,1,0:T(8,128)} %neg.30), kind=kLoop, calls=%fused_computation.72 | loop fusion | flops 524288 | bytes 3276800 | tf_op jit(solution)/shard_map/mul | solution.py:729
  180.4 2.6 copy.156
  183.0 1.3 fusion.24
  184.4 1.2 fusion.23
  185.8 0.8 copy-done.3
  186.9 0.6 maximum_bitcast_fusion.in_ref
  187.5 8.8 %small_sum.5 = f32[48,256]{1,0:T(8,128)} custom-call(f32[48,256]{1,0:T(8,128)} %maximum_bitcast_fusion.in_ref), custom_call_target="tpu_custom_call" | custom-call | tf_op jit(solution)/shard_map/small_sum/pallas_call | solution.py:366
  196.3 0.8 fusion.61
  197.2 0.9 copy.160.refs_1_
  198.6 0.7 pad_maximum_fusion.3
  199.4 0.8 fusion.31
  200.4 0.9 pad_maximum_fusion.2.refs_0_
  201.3 1.1 fusion.12
  202.4 3.9 %convolution_convert_fusion = bf16[768,2048]{1,0:T(8,128)(2,1)} fusion(bf16[256,768]{0,1:T(8,128)(2,1)S(1)} %bitcast.213, bf16[256,8192]{1,0:T(8,128)(2,1)} %bitcast.262, s32[]{:T(128)S(6)} %select_n.11), kind=kOutput, calls=%fused_computation.9 | convolution fusion | flops 806879232 | bytes 4587524 | tf_op jit(solution)/shard_map/dot_general | solution.py:695
  206.4 66.6 %finish_all.1 = (bf16[64,8192]{1,0:T(8,128)(2,1)}, f32[96,2048]{1,0:T(8,128)}, f32[32,1024]{1,0:T(8,128)}, f32[64,256]{1,0:T(8,128)}) custom-call(bf16[256,1536]{1,0:T(8,128)(2,1)} %pad_maximum_fusion.2.refs_0_, bf16[256,768]{1,0:T(8,128)(2,1)} %copy.160.refs_1_, bf16[768,2048]{1,0:T(8,128)(2,1)} %bitcast.219, bf16[8192,1024]{1,0:T(8,128)(2,1)} %refs_3_.3, ...), custom_call_target="tpu_custom_call" | custom-call | tf_op jit(solution)/shard_map/finish_all/pallas_call | solution.py:650
  273.0 1.0 slice.96
  274.1 0.9 reshape.358
  274.9 1.5 slice.95
  276.5 2.3 copy.214
  278.7 0.9 copy.215
  279.6 0.7 copy.216
  280.3 0.6 copy.217
  (111 shorter events, 5.3 us)
Async XLA Ops:
  7.2 54.8 %copy-start.34 = (s32[1,8]{1,0:T(1,128)S(1)}, s32[1,8]{1,0:T(1,128)}, u32[]{:S(2)}) copy-start(s32[1,8]{1,0:T(1,128)} %param.14) | copy-start | bytes 100
  7.2 55.0 %copy-start.33 = (s32[1,8]{1,0:T(1,128)S(1)}, s32[1,8]{1,0:T(1,128)}, u32[]{:S(2)}) copy-start(s32[1,8]{1,0:T(1,128)} %param.15) | copy-start | bytes 100
  7.2 110.6 %all-gather.2.cloned.1.call-start = ((), (), s32[]{:S(2)}) async-start(), calls=%async_computation.2 | async-start | bytes 5242880 | tf_op jit(solution)/shard_map/all_gather | solution.py:829
  61.9 211.1 %reduce-scatter.5.cloned.1.call-start = ((), (), s32[]{:S(2)}) async-start(), calls=%async_computation.4 | async-start | bytes 1769472 | tf_op jit(solution)/shard_map/reduce_scatter | solution.py:954
  62.3 3.9 %copy-start.30 = (f32[256,16]{0,1:T(8,128)}, f32[256,16]{0,1:T(8,128)S(1)}, u32[]{:S(2)}) copy-start(f32[256,16]{0,1:T(8,128)S(1)} %get-tuple-element.61) | copy-start | bytes 49156
  62.3 10.7 %copy-start.26 = (bf16[8,2,2,16,256]{4,3,2,1,0:T(8,128)(2,1)S(1)}, bf16[8,2,2,16,256]{4,3,2,1,0:T(8,128)(2,1)}, u32[]{:S(2)}) copy-start(bf16[8,2,2,16,256]{4,3,2,1,0:T(8,128)(2,1)} %get-tuple-element.24) | copy-start | bytes 786436
  66.2 10.8 %copy-start.22 = (bf16[8,2,16,1024]{3,2,1,0:T(8,128)(2,1)S(1)}, bf16[8,2,16,1024]{3,2,1,0:T(8,128)(2,1)}, u32[]{:S(2)}) copy-start(bf16[8,2,16,1024]{3,2,1,0:T(8,128)(2,1)} %get-tuple-element.25) | copy-start | bytes 1572868
  73.1 0.7 copy-start.6
  73.1 3.9 %copy-start.10 = (bf16[256,16,16]{0,2,1:T(8,128)(2,1)}, bf16[256,16,16]{0,2,1:T(8,128)(2,1)S(1)}, u32[]{:S(2)}) copy-start(bf16[256,16,16]{0,2,1:T(8,128)(2,1)S(1)} %get-tuple-element.55) | copy-start | bytes 393220
  73.1 5.5 %copy-start.8 = (bf16[256,16,16]{0,2,1:T(8,128)(2,1)}, bf16[256,16,16]{0,2,1:T(8,128)(2,1)S(1)}, u32[]{:S(2)}) copy-start(bf16[256,16,16]{0,2,1:T(8,128)(2,1)S(1)} %get-tuple-element.56) | copy-start | bytes 393220
  82.9 1.9 copy-start.5
  83.3 84.0 %copy-start.1 = (f32[256,128]{0,1:T(8,128)}, f32[256,128]{0,1:T(8,128)S(1)}, u32[]{:S(2)}) copy-start(f32[256,128]{0,1:T(8,128)S(1)} %get-tuple-element.48) | copy-start | bytes 393220
  84.8 0.9 copy-start.27
  85.7 5.1 %copy-start.24 = (bf16[256,2,4,128]{0,3,2,1:T(8,128)(2,1)}, bf16[256,2,4,128]{0,3,2,1:T(8,128)(2,1)S(1)}, u32[]{:S(2)}) copy-start(bf16[256,2,4,128]{0,3,2,1:T(8,128)(2,1)S(1)} %fusion.33) | copy-start | bytes 1572868
  85.7 3.1 %copy-start.25 = (bf16[256,2,128]{2,1,0:T(2,128)(2,1)S(1)}, bf16[256,2,128]{2,1,0:T(2,128)(2,1)}, u32[]{:S(2)}) copy-start(bf16[256,2,128]{2,1,0:T(2,128)(2,1)} %convert_element_type.141) | copy-start | bytes 393220
  88.7 2.0 copy-start.20
  88.8 2.0 copy-start.31
  90.8 27.1 %copy-start.12 = (bf16[8,2,4,8192]{3,2,1,0:T(4,128)(2,1)S(1)}, bf16[8,2,4,8192]{3,2,1,0:T(4,128)(2,1)}, u32[]{:S(2)}) copy-start(bf16[8,2,4,8192]{3,2,1,0:T(4,128)(2,1)} %get-tuple-element.28) | copy-start | bytes 3145732
  133.7 1.2 copy-start.13
  133.7 142.8 %reduce-scatter.3.cloned.1.call-start = ((), (), s32[]{:S(2)}) async-start(), calls=%async_computation.3 | async-start | bytes 5242880 | tf_op jit(solution)/shard_map/reduce_scatter | solution.py:922
  146.8 1.1 copy-start.21
  162.3 0.7 copy-start.18
  180.4 5.1 %copy-start.2 = (f32[256,128]{0,1:T(8,128)S(1)}, f32[256,128]{0,1:T(8,128)}, u32[]{:S(2)}) copy-start(f32[256,128]{0,1:T(8,128)} %copy-done.1) | copy-start | bytes 393220
  183.0 2.5 copy-start
  184.3 2.2 copy-start.23
  184.3 2.2 copy-start.32
  185.8 0.8 copy-start.3
  186.6 11.5 %copy-start.7 = (bf16[256,16,16]{0,2,1:T(8,128)(2,1)S(1)}, bf16[256,16,16]{0,2,1:T(8,128)(2,1)}, u32[]{:S(2)}) copy-start(bf16[256,16,16]{0,2,1:T(8,128)(2,1)} %copy-done.6) | copy-start | bytes 393220
  186.6 11.5 %copy-start.19 = (bf16[2,128,256]{2,1,0:T(8,128)(2,1)S(1)}, bf16[2,128,256]{2,1,0:T(8,128)(2,1)}, u32[]{:S(2)}) copy-start(bf16[2,128,256]{2,1,0:T(8,128)(2,1)} %copy-done.18) | copy-start | bytes 393220
  186.6 11.8 %copy-start.9 = (bf16[256,16,16]{0,2,1:T(8,128)(2,1)S(1)}, bf16[256,16,16]{0,2,1:T(8,128)(2,1)}, u32[]{:S(2)}) copy-start(bf16[256,16,16]{0,2,1:T(8,128)(2,1)} %copy-done.8) | copy-start | bytes 393220
  186.9 12.4 %copy-start.15 = (f32[256,128]{1,0:T(8,128)S(1)}, f32[256,128]{1,0:T(8,128)}, u32[]{:S(2)}) copy-start(f32[256,128]{1,0:T(8,128)} %copy.147) | copy-start | bytes 393220
  199.4 0.9 copy-start.16
  199.4 1.0 copy-start.17
  199.4 1.9 copy-start.4
  199.4 1.9 copy-start.11
  273.0 5.7 %copy-start.14 = (f32[96,2048]{1,0:T(8,128)S(1)}, f32[96,2048]{1,0:T(8,128)}, u32[]{:S(2)}) copy-start(f32[96,2048]{1,0:T(8,128)} %get-tuple-element.30) | copy-start | bytes 2359300
  274.0 5.6 %copy-start.28 = (f32[32,1024]{1,0:T(8,128)S(1)}, f32[32,1024]{1,0:T(8,128)}, u32[]{:S(2)}) copy-start(f32[32,1024]{1,0:T(8,128)} %get-tuple-element.31) | copy-start | bytes 393220
  274.9 5.3 %copy-start.29 = (f32[64,256]{1,0:T(8,128)S(1)}, f32[64,256]{1,0:T(8,128)}, u32[]{:S(2)}) copy-start(f32[64,256]{1,0:T(8,128)} %get-tuple-element.32) | copy-start | bytes 196612
Sparse Core Ops, SparseCore 0:
  62.1 55.7 all-gather.1
  133.8 30.8 reduce-scatter.4
  168.3 62.3 reduce-scatter.2
